TPU v7x, 32 devices: a whole 2x2x4 slice. The times are simulated.
32 devices in a mesh: seq: 8 (over y, x, core), dp: 4 (over z).
Axes of the slice: x: 2, y: 2, z: 4, core: 2. Of those that a mesh axis runs over, the one named last changes fastest.
Arguments:
- tokens: bfloat16 [16384, 1024], P(('dp', 'seq')), parts along dimension 0, may hold values from -6 to 6
- norm_gain: float32 [1024], replicated, may hold values from 0.25 to 1.75
- query_weight: bfloat16 [1024, 1024], replicated
- key_weight: bfloat16 [1024, 1024], replicated
- value_weight: bfloat16 [1024, 1024], replicated, may hold values from -0.1875 to 0.1875
- out_weight: bfloat16 [1024, 1024], replicated, may hold values from -0.1875 to 0.1875
- random_blocks: int32 [256, 3], P('dp'), parts along dimension 0, may hold values from 0 to 63, as said below
- bucket_id: int32 [1], replicated, may hold values from 0 to 7
- global_positions: int32 [8, 128], replicated, may hold values from 0 to 4095, as said below
Outputs:
- layer_out: bfloat16 [16384, 1024], P(('dp', 'seq')), parts along dimension 0
There are 4 independent parts, one for each index of `dp`. A program takes and returns all parts, laid end to end along the dimension named above; an argument that names none is the same for every part. Nothing has to cross between parts.
Inputs may be any that keep to these rules, and one draw needn't show every extreme that they name: `random_blocks`: each row lists 3 block numbers. For the query blocks of one device (aligned runs of 8 rows) at most 3 of the listed blocks lie within the tokens of any one device, and exactly 3 for some device. A block may be listed more than once. `global_positions`: each row holds 128 distinct positions in rising order.
All inputs are finite; a program needn't handle non-finite values.
Results may differ from a plain program's by a relative error of at most 0.0089.
Values may be sent and summed in bfloat16 or wider, within the bound.
No kernel may reach another device: no remote copies, remote signals or barrier semaphores. Data moves between devices by JAX's collectives and lax.ppermute only.
A program may use at most 128 MiB of HBM per device.

v0:
```python
import jax
import jax.numpy as jnp
from jax import lax
from jax.sharding import PartitionSpec as P

HEADS = 16
HDIM = 64
BLOCK = 64
RAND = 3
NGLOB = 128


def with_halo(block, sides, width):
    for axis, dim in sides:
        count = lax.axis_size(axis)
        forward = [(i, i + 1) for i in range(count - 1)]
        forward.append((count - 1, 0))
        backward = [(target, source) for source, target in forward]
        low = lax.ppermute(
            lax.slice_in_dim(block, block.shape[dim] - width, None, axis=dim), axis, forward
        )
        high = lax.ppermute(lax.slice_in_dim(block, 0, width, axis=dim), axis, backward)
        block = jnp.concatenate([low, block, high], axis=dim)
    return block


def combined_all(value, axis, join):
    pieces = jax.tree.map(lambda part: lax.all_gather(part, axis), value)
    head = jax.tree.map(lambda part: part[0], pieces)
    tail = jax.tree.map(lambda part: part[1:], pieces)
    running, _ = lax.scan(lambda running, piece: (join(running, piece), None), head, tail)
    return running


def layer_norm(tokens, norm_gain):
    values = tokens.astype(jnp.float32)
    center = values - jnp.mean(values, axis=-1, keepdims=True)
    spread = jnp.mean(center * center, axis=-1, keepdims=True)
    return (center * lax.rsqrt(spread + 1e-05) * norm_gain).astype(jnp.bfloat16)


def combine_rows(first, second):
    top_score = jnp.maximum(first[0], second[0])
    first_factor = jnp.exp(first[0] - top_score)
    second_factor = jnp.exp(second[0] - top_score)
    total = first[1] * first_factor + second[1] * second_factor
    weighted = first[2] * first_factor[..., None] + second[2] * second_factor[..., None]
    return (top_score, total, weighted)


def body(
    tokens,
    norm_gain,
    query_weight,
    key_weight,
    value_weight,
    out_weight,
    random_blocks,
    bucket_id,
    global_positions,
):
    shards = lax.axis_size("seq")
    device = lax.axis_index("seq")
    rows_here = tokens.shape[0]
    width = tokens.shape[1]
    local_blocks = rows_here // BLOCK
    slots = local_blocks * RAND
    capacity = (slots + shards - 1) // shards
    scale = HDIM ** (-0.5)
    normed = layer_norm(tokens, norm_gain)
    queries = jnp.dot(normed, query_weight, preferred_element_type=jnp.float32).astype(jnp.bfloat16)
    key_rows = jnp.dot(normed, key_weight, preferred_element_type=jnp.float32).astype(jnp.bfloat16)
    value_rows = jnp.dot(normed, value_weight, preferred_element_type=jnp.float32).astype(
        jnp.bfloat16
    )
    paired = jnp.concatenate([key_rows, value_rows], axis=1)
    widened = with_halo(paired, (("seq", 0),), BLOCK)
    wide_blocks = widened.reshape(local_blocks + 2, BLOCK, 2 * width)
    window = jnp.stack([wide_blocks[:-2], wide_blocks[1:-1], wide_blocks[2:]], axis=1)
    window = window.reshape(local_blocks, 3 * BLOCK, 2 * width)
    table = random_blocks.reshape(shards, slots)
    my_table = lax.dynamic_slice_in_dim(table, device, 1, 0)[0]
    source = table // local_blocks
    inner = table % local_blocks
    match = (source == device).astype(jnp.int32)
    rank = jnp.cumsum(match, axis=1) - 1
    slot_iota = jnp.arange(capacity, dtype=jnp.int32)
    select = (match[:, :, None] == 1) & (rank[:, :, None] == slot_iota[None, None, :])
    send_index = jnp.sum(jnp.where(select, inner[:, :, None], 0), axis=1)
    blocks_here = paired.reshape(local_blocks, BLOCK, 2 * width)
    outgoing = blocks_here[send_index]
    incoming = lax.all_to_all(outgoing, "seq", split_axis=0, concat_axis=0, tiled=True)
    incoming = incoming.reshape(shards * capacity, BLOCK, 2 * width)
    my_source = my_table // local_blocks
    slot_order = jnp.arange(slots, dtype=jnp.int32)
    same = (my_source[:, None] == my_source[None, :]) & (slot_order[None, :] < slot_order[:, None])
    my_rank = jnp.sum(same.astype(jnp.int32), axis=1)
    random_rows = incoming[my_source * capacity + my_rank]
    random_rows = random_rows.reshape(local_blocks, RAND * BLOCK, 2 * width)
    positions = global_positions[bucket_id[0]]
    local_position = positions - device * rows_here
    selector = (local_position[:, None] == jnp.arange(rows_here, dtype=jnp.int32)[None, :]).astype(
        jnp.bfloat16
    )
    global_normed = lax.psum(
        jnp.dot(selector, normed, preferred_element_type=jnp.float32).astype(jnp.bfloat16), "seq"
    )
    global_queries = jnp.dot(
        global_normed, query_weight, preferred_element_type=jnp.float32
    ).astype(jnp.bfloat16)
    global_keys = jnp.dot(global_normed, key_weight, preferred_element_type=jnp.float32).astype(
        jnp.bfloat16
    )
    global_values = jnp.dot(global_normed, value_weight, preferred_element_type=jnp.float32).astype(
        jnp.bfloat16
    )
    global_paired = jnp.concatenate([global_keys, global_values], axis=1)
    global_broad = jnp.broadcast_to(global_paired[None], (local_blocks, NGLOB, 2 * width))
    key_set = jnp.concatenate([window, random_rows, global_broad], axis=1)
    count = key_set.shape[1]
    key_part = key_set[:, :, :width].reshape(local_blocks, count, HEADS, HDIM)
    value_part = key_set[:, :, width:].reshape(local_blocks, count, HEADS, HDIM)
    query_blocks = queries.reshape(local_blocks, BLOCK, HEADS, HDIM)
    scores = (
        jnp.einsum("bqhd,bkhd->bhqk", query_blocks, key_part, preferred_element_type=jnp.float32)
        * scale
    )
    top_score = jnp.max(scores, axis=-1, keepdims=True)
    expo = jnp.exp(scores - top_score)
    probs = (expo / jnp.sum(expo, axis=-1, keepdims=True)).astype(jnp.bfloat16)
    sparse_out = jnp.einsum(
        "bhqk,bkhd->bqhd", probs, value_part, preferred_element_type=jnp.float32
    )
    sparse_out = sparse_out.reshape(rows_here, width).astype(jnp.bfloat16)
    global_heads = global_queries.reshape(NGLOB, HEADS, HDIM)
    local_keys = key_rows.reshape(rows_here, HEADS, HDIM)
    local_values = value_rows.astype(jnp.float32).reshape(rows_here, HEADS, HDIM)
    global_scores = (
        jnp.einsum("qhd,khd->hqk", global_heads, local_keys, preferred_element_type=jnp.float32)
        * scale
    )
    global_top = jnp.max(global_scores, axis=-1)
    global_expo = jnp.exp(global_scores - global_top[..., None])
    global_total = jnp.sum(global_expo, axis=-1)
    global_weighted = jnp.einsum(
        "hqk,khd->hqd", global_expo, local_values, precision=lax.Precision.HIGHEST
    )
    merged = combined_all((global_top, global_total, global_weighted), "seq", combine_rows)
    global_out = merged[2] / merged[1][..., None]
    global_out = jnp.transpose(global_out, (1, 0, 2)).reshape(NGLOB, width).astype(jnp.bfloat16)
    placed = jnp.dot(selector.T, global_out, preferred_element_type=jnp.float32).astype(
        jnp.bfloat16
    )
    owned_row = jnp.sum(selector.astype(jnp.float32), axis=0) > 0.5
    mixed = jnp.where(owned_row[:, None], placed, sparse_out)
    return jnp.dot(mixed, out_weight, preferred_element_type=jnp.float32).astype(jnp.bfloat16)


def solution(mesh):
    placed = (P(("dp", "seq"), None), P(), P(), P(), P(), P(), P("dp", None), P(), P())
    return jax.shard_map(
        body, mesh=mesh, in_specs=placed, out_specs=P(("dp", "seq"), None), check_vma=False
    )
```

profile of v0, /device:TPU:0, one launch (start us, length us, event | category | flops | bytes accessed | tf_op | source)
XLA Modules:
  0.0 269.2 jit_solution(3711062153873412040)
XLA Ops:
  6.5 1.6 convert_reduce_fusion
  8.1 1.6 fusion.15
  9.8 3.1 %convolution_convert_fusion.4 = bf16[512,1024]{1,0:T(8,128)(2,1)S(1)} fusion(bf16[1024,1024]{1,0:T(8,128)(2,1)} %param.14, bf16[512,1024]{1,0:T(8,128)(2,1)S(1)} %copy-done.7, f32[1024]{0:T(1024)S(1)} %copy-done.16, f32[512]{0:T(512)S(1)} %add_rsqrt_fusion, f32[512]{0:T(512)S(1)} %broadcast_multiply_fusion), kind=kOutput, calls=%fused_computation.51 | convolution fusion | flops 1076887552 | bytes 4202496 | tf_op jit(solution)/shard_map/dot_general | solution.py:72
  15.6 2.9 %collective-permute-start.1 = (bf16[64,2048]{1,0:T(8,128)(2,1)}, bf16[64,2048]{1,0:T(8,128)(2,1)}, u32[]{:S(2)}, u32[]{:S(2)}) collective-permute-start(bf16[64,2048]{1,0:T(8,128)(2,1)} %get-tuple-element.99), channel_id=1, source_target_pairs={{4,0},{8,4},{12,8},{16,12},{20,16},{24,20},{28,24},{0,28},{5,1},{9... | collective-permute-start | bytes 786440 | tf_op jit(solution)/shard_map/ppermute | solution.py:22
  19.2 3.7 %collective-permute-done = bf16[64,2048]{1,0:T(8,128)(2,1)S(1)} collective-permute-done((bf16[64,2048]{1,0:T(8,128)(2,1)}, bf16[64,2048]{1,0:T(8,128)(2,1)S(1)}, u32[]{:S(2)}, u32[]{:S(2)}) %collective-permute-start) | collective-permute-done | bytes 262176 | tf_op jit(solution)/shard_map/ppermute | solution.py:19
  22.8 1.6 collective-permute-done.1
  24.5 6.7 %pad_maximum_fusion.5 = (bf16[512,2048]{1,0:T(8,128)(2,1)}, bf16[512,2048]{1,0:T(8,128)(2,1)}, bf16[512,2048]{1,0:T(8,128)(2,1)}) fusion(bf16[64,2048]{1,0:T(8,128)(2,1)S(1)} %collective-permute-done, bf16[512,1024]{1,0:T(8,128)(2,1)S(1)} %convolution_convert_fusion.3, bf16[512,1024]{1,0:T(8,128)(2,1)} %copy-done.3, bf16[64,2048]{1,0:T(8,128)(2,1)} %collective-permute-done.1), kind=kLoop, calls=%fused_computation.39 | loop fusion | flops 16777216 | bytes 8912896 | tf_op jit(solution)/shard_map/concatenate | solution.py:23
  31.2 6.0 %gather_fusion = bf16[24,64,2048]{2,1,0:T(8,128)(2,1)} fusion(bf16[8,64,2048]{2,1,0:T(8,128)(2,1)} %bitcast.101, s32[1024]{0:T(1024)S(1)} %pad_clamp_fusion.1), kind=kCustom, calls=%fused_computation | custom fusion | bytes 12583008 | tf_op jit(solution)/shard_map/gather | solution.py:91
  37.2 4.7 %all-to-all-start = ((bf16[8,3,64,2048]{3,2,1,0:T(8,128)(2,1)}), bf16[8,3,64,2048]{3,2,1,0:T(8,128)(2,1)}, u32[]{:S(2)}, u32[]{:S(2)}) async-start(bf16[8,3,64,2048]{3,2,1,0:T(8,128)(2,1)} %bitcast.104), calls=%async_computation | async-start | bytes 12582912 | tf_op jit(solution)/shard_map/all_to_all | solution.py:92
  43.4 2.5 convolution_convert_fusion.8
  46.3 3.5 %convolution_convert_fusion.2 = bf16[512,1024]{1,0:T(8,128)(2,1)} fusion(bf16[1024,1024]{1,0:T(8,128)(2,1)S(1)} %copy-done, bf16[512,1024]{1,0:T(8,128)(2,1)} %param.11, f32[1024]{0:T(1024)S(1)} %copy-done.16, f32[512]{0:T(512)S(1)} %add_rsqrt_fusion, f32[512]{0:T(512)S(1)} %broadcast_multiply_fusion), kind=kOutput, calls=%fused_computation.49 | convolution fusion | flops 1076887552 | bytes 4202496 | tf_op jit(solution)/shard_map/dot_general | solution.py:71
  49.9 2.3 copy.50
  53.5 4.0 %reshape.283 = bf16[8,64,16,64]{3,2,1,0:T(8,128)(2,1)} reshape(bf16[512,1024]{1,0:T(8,128)(2,1)} %convolution_convert_fusion.2) | data formatting | bytes 2097152 | tf_op jit(solution)/shard_map/reshape | solution.py:123
  57.5 71.0 %all-reduce.2.cloned.1.call-done = bf16[128,1024]{1,0:T(8,128)(2,1)} async-done(((bf16[128,1024]{1,0:T(8,128)(2,1)}), bf16[128,1024]{1,0:T(8,128)(2,1)}) %all-reduce.2.cloned.1.call-update) | async-done | bytes 262160 | tf_op jit(solution)/shard_map/psum | solution.py:105
  132.1 8.7 %all-gather.1 = f32[128,128]{1,0:T(8,128)S(1)} all-gather(f32[16,128]{1,0:T(8,128)S(1)} %fusion.10), channel_id=3, replica_groups=mesh['seq'=8,'dp'=4] {'seq'}, dimensions={0}, use_global_device_ids=true | all-gather | bytes 73728 | tf_op jit(solution)/shard_map/all_gather | solution.py:28
  140.8 8.9 %all-gather = f32[128,128]{1,0:T(8,128)S(1)} all-gather(f32[16,128]{1,0:T(8,128)S(1)} %get-tuple-element.102), channel_id=2, replica_groups=mesh['seq'=8,'dp'=4] {'seq'}, dimensions={0}, use_global_device_ids=true | all-gather | bytes 73728 | tf_op jit(solution)/shard_map/all_gather | solution.py:28
  149.8 4.0 %fusion.9 = f32[16,128,64]{1,2,0:T(8,128)} fusion(bf16[512,16,64]{0,2,1:T(8,128)(2,1)S(1)} %bitcast.111, f32[16,128,512]{2,1,0:T(8,128)S(1)} %get-tuple-element.103, f32[16,128]{1,0:T(8,128)S(1)} %get-tuple-element.102), kind=kOutput, calls=%fused_computation.22 | convolution fusion | flops 807403520 | bytes 5775360 | tf_op jit(solution)/shard_map/hqk,khd->hqd/dot_general | solution.py:145
  153.8 2.2 convolution_convert_fusion.5
  156.0 2.2 convolution_convert_fusion.6
  158.4 3.3 %pad_maximum_fusion.1 = bf16[8,3,64,2048]{3,2,1,0:T(8,128)(2,1)} fusion(bf16[8,1,64,2048]{3,2,1,0:T(8,128)(2,1)S(1)} %bitcast.110, bf16[8,1,64,2048]{3,2,1,0:T(8,128)(2,1)S(1)} %bitcast.102, bf16[8,1,64,2048]{3,2,1,0:T(8,128)(2,1)S(1)} %bitcast.109), kind=kLoop, calls=%fused_computation.19 | loop fusion | flops 6291456 | bytes 12582912 | tf_op jit(solution)/shard_map/stack | solution.py:79
  161.7 7.4 %gather_fusion.1 = bf16[24,64,2048]{2,1,0:T(8,128)(2,1)} fusion(bf16[24,64,2048]{2,1,0:T(8,128)(2,1)} %bitcast.23, s32[1024]{0:T(1024)S(1)} %pad_clamp_fusion), kind=kCustom, calls=%fused_computation.1 | custom fusion | bytes 12583008 | tf_op jit(solution)/shard_map/gather | solution.py:98
  169.6 7.8 %pad_maximum_fusion = bf16[8,512,2048]{2,1,0:T(8,128)(2,1)S(1)} fusion(bf16[8,128,2048]{2,1,0:T(8,128)(2,1)S(1)} %broadcast_in_dim.22, bf16[8,192,2048]{2,1,0:T(8,128)(2,1)} %bitcast.106, bf16[8,192,2048]{2,1,0:T(8,128)(2,1)} %bitcast.105), kind=kLoop, calls=%fused_computation.12 | loop fusion | flops 50331648 | bytes 33554432 | tf_op jit(solution)/shard_map/concatenate | solution.py:119
  177.3 6.3 %fusion.53 = (bf16[8,512,1024]{2,1,0:T(8,128)(2,1)}, bf16[8,512,1024]{2,1,0:T(8,128)(2,1)}) fusion(bf16[8,512,2048]{2,1,0:T(8,128)(2,1)S(1)} %pad_maximum_fusion), kind=kLoop, calls=%fused_computation.113 | loop fusion | bytes 33554432 | tf_op jit(solution)/shard_map/slice | solution.py:121
  183.6 11.5 %copy.61 = bf16[8,512,1024]{1,2,0:T(8,128)(2,1)} copy(bf16[8,512,1024]{2,1,0:T(8,128)(2,1)} %get-tuple-element.93) | data formatting | bytes 16777216 | tf_op jit(solution)/shard_map/slice | solution.py:121
  195.1 11.6 %copy.60 = bf16[8,512,1024]{1,2,0:T(8,128)(2,1)} copy(bf16[8,512,1024]{2,1,0:T(8,128)(2,1)} %get-tuple-element.94) | data formatting | bytes 16777216 | tf_op jit(solution)/shard_map/slice | solution.py:122
  206.7 10.5 %fusion.54 = (f32[8,16,64]{2,1,0:T(8,128)S(1)}, f32[8,16,64,512]{3,2,1,0:T(8,128)}) fusion(bf16[8,512,16,64]{1,3,2,0:T(8,128)(2,1)} %bitcast.103, bf16[8,64,16,64]{3,2,1,0:T(8,128)(2,1)S(1)} %copy-done.6), kind=kOutput, calls=%fused_computation.114 | convolution fusion | flops 549454336 | bytes 26247168 | tf_op jit(solution)/shard_map/sub | solution.py:129
  217.1 10.9 %convert_bitcast_fusion = bf16[8,64,16,64]{1,3,2,0:T(8,128)(2,1)} fusion(bf16[8,512,16,64]{1,3,2,0:T(8,128)(2,1)} %bitcast.108, f32[8,16,64,512]{3,2,1,0:T(8,128)} %get-tuple-element.101, f32[8,16,64]{2,1,0:T(8,128)S(1)} %get-tuple-element.100), kind=kOutput, calls=%fused_computation.41 | convolution fusion | flops 545783808 | bytes 26247168 | tf_op jit(solution)/shard_map/bhqk,bkhd->bqhd/dot_general | solution.py:131
  228.1 3.6 %copy.63 = bf16[8,64,16,64]{3,2,1,0:T(8,128)(2,1)S(1)} copy(bf16[8,64,16,64]{1,3,2,0:T(8,128)(2,1)} %convert_bitcast_fusion) | data formatting | bytes 2097152 | tf_op jit(solution)/shard_map/convert_element_type | solution.py:134
  231.7 2.3 convert_element_type.95
  235.4 4.3 %slice.69 = f32[112,128,64]{1,2,0:T(8,128)} slice(f32[128,128,64]{1,2,0:T(8,128)} %all-gather.5.cloned.1.call-done), slice={[16:128], [0:128], [0:64]} | slice | bytes 7340032 | tf_op jit(solution)/shard_map/slice | solution.py:30
  239.8 17.1 %while.14 = (s32[]{:T(128)}, f32[16,128]{1,0:T(8,128)S(1)}, f32[16,128]{1,0:T(8,128)S(1)}, f32[16,128,64]{2,1,0:T(8,128)S(1)}, f32[7,16,128]{2,1,0:T(8,128)S(1)}...) while((s32[]{:T(128)}, f32[16,128]{1,0:T(8,128)S(1)}, f32[16,128]{1,0:T(8,128)S(1)}, ...), condition=%wide.region_7.8_spmd, body=%wide.region_6.7_spmd.sunk | while | flops 405506 | bytes 3752029 | solution.py:31
  258.1 4.2 %convolution_convert_fusion.1 = bf16[512,1024]{1,0:T(8,128)(2,1)} fusion(bf16[1024,1024]{1,0:T(8,128)(2,1)} %param.16, bf16[512,1024]{1,0:T(8,128)(2,1)S(1)} %copy-done.12, bf16[128,1024]{0,1:T(8,128)(2,1)S(1)} %bitcast.114, pred[512]{0:T(512)(128)(4,1)S(1)} %broadcast_compare_fusion.1, s32[128]{0:T(128)S(1)} %subtract_bitcast_fusion), kind=kOutput, calls=%fused_computation.48 | convolution fusion | flops 1209663488 | bytes 4457472 | tf_op jit(solution)/shard_map/dot_general | solution.py:156
  (108 shorter events, 29.6 us)
Async XLA Ops:
  6.5 39.8 %copy-start = (bf16[1024,1024]{1,0:T(8,128)(2,1)S(1)}, bf16[1024,1024]{1,0:T(8,128)(2,1)}, u32[]{:S(2)}) copy-start(bf16[1024,1024]{1,0:T(8,128)(2,1)} %param.13) | copy-start | bytes 6291460
  6.5 3.2 %copy-start.7 = (bf16[512,1024]{1,0:T(8,128)(2,1)S(1)}, bf16[512,1024]{1,0:T(8,128)(2,1)}, u32[]{:S(2)}) copy-start(bf16[512,1024]{1,0:T(8,128)(2,1)} %param.11) | copy-start | bytes 3145732
  6.5 3.3 %copy-start.16 = (f32[1024]{0:T(1024)S(1)}, f32[1024]{0:T(1024)}, u32[]{:S(2)}) copy-start(f32[1024]{0:T(1024)} %param.12) | copy-start | bytes 12292
  9.8 3.1 %copy-start.11 = (bf16[1024,1024]{1,0:T(8,128)(2,1)S(1)}, bf16[1024,1024]{1,0:T(8,128)(2,1)}, u32[]{:S(2)}) copy-start(bf16[1024,1024]{1,0:T(8,128)(2,1)} %param.15) | copy-start | bytes 6291460
  12.9 1.4 copy-start.3
  14.3 4.2 %copy-start.15 = (s32[64,3]{0,1:T(4,128)S(1)}, s32[64,3]{0,1:T(4,128)}, u32[]{:S(2)}) copy-start(s32[64,3]{0,1:T(4,128)} %param.17) | copy-start | bytes 2308
  15.1 7.7 %collective-permute-start = (bf16[64,2048]{1,0:T(8,128)(2,1)}, bf16[64,2048]{1,0:T(8,128)(2,1)S(1)}, u32[]{:S(2)}, u32[]{:S(2)}) collective-permute-start(bf16[64,2048]{1,0:T(8,128)(2,1)} %get-tuple-element.98), channel_id=1, source_target_pairs={{0,4},{4,8},{8,12},{12,16},{16,20},{20,24},{24,28},{28,0},{1,5},{5... | collective-permute-start | bytes 786440 | tf_op jit(solution)/shard_map/ppermute | solution.py:19
  15.6 8.9 %collective-permute-start.1 = (bf16[64,2048]{1,0:T(8,128)(2,1)}, bf16[64,2048]{1,0:T(8,128)(2,1)}, u32[]{:S(2)}, u32[]{:S(2)}) collective-permute-start(bf16[64,2048]{1,0:T(8,128)(2,1)} %get-tuple-element.99), channel_id=1, source_target_pairs={{4,0},{8,4},{12,8},{16,12},{20,16},{24,20},{28,24},{0,28},{5,1},{9... | collective-permute-start | bytes 786440 | tf_op jit(solution)/shard_map/ppermute | solution.py:22
  37.2 124.4 %all-to-all-start = ((bf16[8,3,64,2048]{3,2,1,0:T(8,128)(2,1)}), bf16[8,3,64,2048]{3,2,1,0:T(8,128)(2,1)}, u32[]{:S(2)}, u32[]{:S(2)}) async-start(bf16[8,3,64,2048]{3,2,1,0:T(8,128)(2,1)} %bitcast.104), calls=%async_computation | async-start | bytes 12582912 | tf_op jit(solution)/shard_map/all_to_all | solution.py:92
  42.0 86.5 %all-reduce.2.cloned.1.call-start = ((), (), s32[]{:S(2)}) async-start(), calls=%async_computation.1 | async-start | bytes 524288 | tf_op jit(solution)/shard_map/psum | solution.py:105
  45.9 188.0 %all-gather.5.cloned.1.call-start = ((), (), s32[]{:S(2)}) async-start(), calls=%async_computation.2 | async-start | bytes 4718592 | tf_op jit(solution)/shard_map/all_gather | solution.py:28
  57.5 72.5 %copy-start.9 = (bf16[512,1024]{0,1:T(8,128)(2,1)S(1)}, bf16[512,1024]{0,1:T(8,128)(2,1)}, u32[]{:S(2)}) copy-start(bf16[512,1024]{0,1:T(8,128)(2,1)} %copy.50) | copy-start | bytes 3145732
  130.9 18.9 %copy-start.8 = (bf16[512,1024]{0,1:T(8,128)(2,1)S(1)}, bf16[512,1024]{0,1:T(8,128)(2,1)}, u32[]{:S(2)}) copy-start(bf16[512,1024]{0,1:T(8,128)(2,1)} %copy.51) | copy-start | bytes 3145732
  140.8 17.4 %copy-start.13 = (f32[128,128]{1,0:T(8,128)}, f32[128,128]{1,0:T(8,128)S(1)}, u32[]{:S(2)}) copy-start(f32[128,128]{1,0:T(8,128)S(1)} %all-gather.1) | copy-start | bytes 196612
  149.8 8.5 %copy-start.14 = (f32[128,128]{1,0:T(8,128)}, f32[128,128]{1,0:T(8,128)S(1)}, u32[]{:S(2)}) copy-start(f32[128,128]{1,0:T(8,128)S(1)} %all-gather) | copy-start | bytes 196612
  149.8 4.0 %copy-start.10 = (bf16[128,1024]{1,0:T(8,128)(2,1)S(1)}, bf16[128,1024]{1,0:T(8,128)(2,1)}, u32[]{:S(2)}) copy-start(bf16[128,1024]{1,0:T(8,128)(2,1)} %all-reduce.2.cloned.1.call-done) | copy-start | bytes 786436
  153.8 4.5 %copy-start.4 = (bf16[512,2048]{1,0:T(8,128)(2,1)S(1)}, bf16[512,2048]{1,0:T(8,128)(2,1)}, u32[]{:S(2)}) copy-start(bf16[512,2048]{1,0:T(8,128)(2,1)} %get-tuple-element.95) | copy-start | bytes 6291460
  153.8 4.5 %copy-start.5 = (bf16[512,2048]{1,0:T(8,128)(2,1)S(1)}, bf16[512,2048]{1,0:T(8,128)(2,1)}, u32[]{:S(2)}) copy-start(bf16[512,2048]{1,0:T(8,128)(2,1)} %get-tuple-element.96) | copy-start | bytes 6291460
  156.0 2.4 copy-start.2
  195.1 11.6 %copy-start.6 = (bf16[8,64,16,64]{3,2,1,0:T(8,128)(2,1)S(1)}, bf16[8,64,16,64]{3,2,1,0:T(8,128)(2,1)}, u32[]{:S(2)}) copy-start(bf16[8,64,16,64]{3,2,1,0:T(8,128)(2,1)} %reshape.283) | copy-start | bytes 3145732
  235.4 4.4 %slice-start = ((f32[128,128]{1,0:T(8,128)}), f32[16,128]{1,0:T(8,128)S(1)}, s32[]{:S(2)}) async-start(f32[128,128]{1,0:T(8,128)} %copy-done.13), calls=%async_computation.3 | async-start | bytes 16384 | tf_op jit(solution)/shard_map/slice | solution.py:29
  235.4 4.3 %slice-start.1 = ((f32[128,128]{1,0:T(8,128)}), f32[16,128]{1,0:T(8,128)S(1)}, s32[]{:S(2)}) async-start(f32[128,128]{1,0:T(8,128)} %copy-done.14), calls=%async_computation.4 | async-start | bytes 16384 | tf_op jit(solution)/shard_map/slice | solution.py:29
  256.9 1.2 copy-start.12
  257.3 5.1 %copy-start.1 = (bf16[1024,1024]{1,0:T(8,128)(2,1)S(1)}, bf16[1024,1024]{1,0:T(8,128)(2,1)}, u32[]{:S(2)}) copy-start(bf16[1024,1024]{1,0:T(8,128)(2,1)} %param.13) | copy-start | bytes 6291460
Sparse Core Ops, SparseCore 0:
  46.0 82.3 all-reduce.1
  153.9 36.7 all-gather.4
where the time goes:
time: 271 us; the launch traced here: 269 us
  waiting for transfers between devices  76.3 us (28%)
  local copies, waits for them, and re-layouts  74.2 us (27%)
  matrix products  46.6 us (17%)
  other arithmetic  31.5 us (12%)
  blocking collectives  17.6 us (6%)
  between operations  14.4 us (5%)
  starting transfers between devices  8.15 us (3%)
    psum x1, waiting for transfers between devices, body(): lax.psum(jnp.dot(selector, normed, preferred_element_type=jnp.float32).as...  71 us
    slice x2, local copies, waits for them, and re-layouts, body(): key_part = key_set[:, :, :width].reshape(local_blocks, count, HEADS, HDIM)  17.8 us
    all_gather x2, blocking collectives, combined_all(): pieces = jax.tree.map(lambda part: lax.all_gather(part, axis), value)  17.6 us
    slice x1, local copies, waits for them, and re-layouts, body(): value_part = key_set[:, :, width:].reshape(local_blocks, count, HEADS, HDIM)  11.6 us
    dot_general x1, matrix products, body(): jnp.einsum('bhqk,bkhd->bqhd', probs, value_part, preferred_element_type=j...  10.9 us
    sub x1, matrix products, body(): expo = jnp.exp(scores - top_score)  10.5 us
    dynamic_slice x14, local copies, waits for them, and re-layouts, combined_all(): lax.scan(lambda running, piece: (join(running, piece), None), head, tail)  9.93 us
    concatenate x1, other arithmetic, body(): key_set = jnp.concatenate([window, random_rows, global_broad], axis=1)  7.77 us
  transfers between devices with their start and end apart: 5, of which 3 were waited for; matrix products, arithmetic and copies ran while one was open for 38% of the time, Pallas kernels for 0%

commit v1 on v0

v1 whole, which is shorter than its diff:
```python
import functools
import math

import jax
import jax.numpy as jnp
from jax import lax
from jax.experimental import pallas as pl
from jax.experimental.pallas import tpu as pltpu
from jax.sharding import PartitionSpec as P

HEADS = 16
HDIM = 64
BLOCK = 64
RAND = 3
NGLOB = 128
GROUP = 4
GW = GROUP * HDIM
TILE = 32
EXP2 = HDIM ** (-0.5) * math.log2(math.e)
F32 = jnp.float32
BF16 = jnp.bfloat16
ANY = pl.BlockSpec(memory_space=pl.ANY)
VMEM = pl.BlockSpec(memory_space=pltpu.VMEM)
SMEM = pl.BlockSpec(memory_space=pltpu.SMEM)


def params(mib):
    return pltpu.CompilerParams(vmem_limit_bytes=mib << 20)


def exchange(value, shift):
    count = lax.axis_size("seq")
    return lax.ppermute(value, "seq", [(i, i ^ shift) for i in range(count)])


def layer_norm(tokens, gain):
    values = tokens.astype(F32)
    center = values - jnp.mean(values, axis=-1, keepdims=True)
    spread = jnp.mean(center * center, axis=-1, keepdims=True)
    return (center * lax.rsqrt(spread + 1e-05) * gain).astype(BF16)


def project_kernel(pieces, weights, *refs):
    token_refs = refs[:pieces]
    gain_ref = refs[pieces]
    weight_refs = refs[pieces + 1 : pieces + 1 + weights]
    outs = refs[pieces + 1 + weights : -5]
    weight_buf, normed, result, in_sem, out_sem = refs[-5:]
    rows, width = normed.shape
    loads = []
    for index, weight in enumerate(weight_refs):
        load = pltpu.make_async_copy(weight, weight_buf.at[index], in_sem.at[index])
        load.start()
        loads.append(load)
    at = 0
    for piece in token_refs:
        step = 128
        for start in range(0, piece.shape[0], step):
            normed[at : at + step, :] = layer_norm(piece[start : start + step, :], gain_ref[...])
            at += step
    stores = []
    for index in range(weights):
        loads[index].wait()
        for column in range(0, width, 256):
            result[index, :, column : column + 256] = jnp.dot(
                normed[...],
                weight_buf[index, :, column : column + 256],
                preferred_element_type=F32,
            ).astype(BF16)
        if index < 2:
            target = outs[0].at[:, index * width : (index + 1) * width]
        else:
            target = outs[1]
        store = pltpu.make_async_copy(result.at[index], target, out_sem.at[index])
        store.start()
        stores.append(store)
    for store in stores:
        store.wait()


def project(pieces, gain, weights):
    rows = sum(piece.shape[0] for piece in pieces)
    width = gain.shape[1]
    count = len(weights)
    shapes = [jax.ShapeDtypeStruct((rows, 2 * width), BF16)]
    if count > 2:
        shapes.append(jax.ShapeDtypeStruct((rows, width), BF16))
    return pl.pallas_call(
        functools.partial(project_kernel, len(pieces), count),
        out_shape=shapes,
        in_specs=[VMEM] * (len(pieces) + 1) + [ANY] * count,
        out_specs=[ANY] * len(shapes),
        scratch_shapes=[
            pltpu.VMEM((count, width, width), BF16),
            pltpu.VMEM((rows, width), BF16),
            pltpu.VMEM((count, rows, width), BF16),
            pltpu.SemaphoreType.DMA((count,)),
            pltpu.SemaphoreType.DMA((count,)),
        ],
        compiler_params=params(24),
        cost_estimate=pl.CostEstimate(
            flops=2 * rows * width * width * count,
            bytes_accessed=2 * width * (width * count + rows * (count + 1)),
            transcendentals=rows,
        ),
        name="project",
    )(*pieces, gain, *weights)


def head_masks(rows, dtype):
    lane = lax.broadcasted_iota(jnp.int32, (rows, GW), 1) // HDIM
    return [(lane == head).astype(dtype) for head in range(GROUP)]


def spread_heads(rows):
    masks = head_masks(rows.shape[0], BF16)
    return jnp.concatenate([rows * mask for mask in masks], axis=0)


def pick_heads(stacked, rows):
    lane = lax.broadcasted_iota(jnp.int32, (rows, GW), 1) // HDIM
    picked = stacked[(GROUP - 1) * rows :]
    for head in range(GROUP - 1):
        picked = jnp.where(lane == head, stacked[head * rows : (head + 1) * rows], picked)
    return picked


def contract_last(left, right):
    return lax.dot_general(
        left, right, (((1,), (1,)), ((), ())), preferred_element_type=F32
    )


def token_positions(devs, index, rows):
    lane = lax.broadcasted_iota(jnp.int32, (1, rows), 1)
    owner = jnp.where(lane < rows // 2, devs[2 * index], devs[2 * index + 1])
    return owner * rows + lane


def gather_global(pos, devs, base, kv_refs, columns):
    total = None
    for index, kv in enumerate(kv_refs):
        select = (pos == token_positions(devs, base + index, kv.shape[0])).astype(BF16)
        part = jnp.dot(select, kv[:, columns], preferred_element_type=F32)
        total = part if total is None else total + part
    return total


def global_partial(count, gq, kv_refs, scores, top_ref, sum_ref, acc_ref):
    width = gq.shape[1]

    def one_tile(tile, carry):
        rows = pl.ds(pl.multiple_of(tile * TILE, TILE), TILE)
        for group in range(width // GW):
            columns = slice(group * GW, (group + 1) * GW)
            values = slice(width + group * GW, width + (group + 1) * GW)
            left = spread_heads(gq[rows, columns])
            at = 0
            for kv in kv_refs:
                keys = kv.shape[0]
                scores[:, at : at + keys] = contract_last(left, kv[:, columns])
                at += keys
            top = jnp.max(scores[...], axis=1, keepdims=True)
            total = jnp.zeros_like(top)
            acc = jnp.zeros((GROUP * TILE, GW), F32)
            at = 0
            for kv in kv_refs:
                keys = kv.shape[0]
                probs = jnp.exp2((scores[:, at : at + keys] - top) * EXP2)
                total += jnp.sum(probs, axis=1, keepdims=True)
                acc += jnp.dot(probs.astype(BF16), kv[:, values], preferred_element_type=F32)
                at += keys
            shape = (GROUP * TILE, GW)
            top_ref[rows, columns] = pick_heads(jnp.broadcast_to(top, shape), TILE)
            sum_ref[rows, columns] = pick_heads(jnp.broadcast_to(total, shape), TILE)
            acc_ref[rows, columns] = pick_heads(acc, TILE)
        return carry

    lax.fori_loop(0, (count + TILE - 1) // TILE, one_tile, 0)


def early_kernel(arrays, *refs):
    devs, count, pos, local, queries = refs[:5]
    kv_refs = refs[5 : 5 + arrays]
    gq, gkv, top, total, acc, scores = refs[5 + arrays :]
    rows, width = queries.shape
    lane = lax.broadcasted_iota(jnp.int32, (1, rows), 1)
    select = (local[...] == lane).astype(BF16)
    for column in range(0, width, 256):
        columns = slice(column, column + 256)
        gq[:, columns] = jnp.dot(
            select, queries[:, columns], preferred_element_type=F32
        ).astype(BF16)
    for column in range(0, 2 * width, 256):
        columns = slice(column, column + 256)
        gkv[:, columns] = gather_global(pos[...], devs, 0, kv_refs, columns).astype(BF16)
    global_partial(count[0], gq, kv_refs, scores, top, total, acc)


def early(devs, count, pos, local, queries, kv):
    rows, width = queries.shape
    keys = rows * len(kv)
    state = jax.ShapeDtypeStruct((NGLOB, width), F32)
    return pl.pallas_call(
        functools.partial(early_kernel, len(kv)),
        out_shape=[
            jax.ShapeDtypeStruct((NGLOB, width), BF16),
            jax.ShapeDtypeStruct((NGLOB, 2 * width), BF16),
            state,
            state,
            state,
        ],
        in_specs=[SMEM, SMEM] + [VMEM] * (3 + len(kv)),
        out_specs=[VMEM] * 5,
        scratch_shapes=[pltpu.VMEM((GROUP * TILE, keys), F32)],
        compiler_params=params(56),
        cost_estimate=pl.CostEstimate(
            flops=8 * TILE * keys * width * 2,
            bytes_accessed=4 * width * keys,
            transcendentals=TILE * HEADS * keys,
        ),
        name="early",
    )(devs, count, pos, local, queries, *kv)


def late_kernel(arrays, late, *refs):
    devs, count, ids, offsets, pos, local_row, queries, gq, gkv = refs[:9]
    top1, sum1, acc1, out_weight = refs[9:13]
    kv_refs = refs[13 : 13 + arrays]
    out = refs[13 + arrays]
    keys, weight, last, mixed, top2, sum2, acc2, placed, scores, sems, sem2 = refs[14 + arrays :]
    rows, width = queries.shape
    blocks = rows // BLOCK
    picks = 3 + RAND
    span = picks * BLOCK

    def copies(block, slot, act):
        for pick in range(picks):
            entry = block * picks + pick
            source = ids[entry]
            start = pl.multiple_of(offsets[entry], BLOCK)
            target = keys.at[slot, pl.ds(pick * BLOCK, BLOCK), :]
            if act == "wait":
                pltpu.make_async_copy(
                    kv_refs[0].at[pl.ds(0, BLOCK), :], target, sems.at[slot, pick]
                ).wait()
                continue
            for index in range(arrays):

                @pl.when(source == index)
                def _():
                    pltpu.make_async_copy(
                        kv_refs[index].at[pl.ds(start, BLOCK), :], target, sems.at[slot, pick]
                    ).start()

    loads = [
        pltpu.make_async_copy(kv_refs[arrays - late + i], last.at[i], sem2.at[i])
        for i in range(late)
    ]
    for load in loads:
        load.start()
    copies(0, 0, "start")
    weight_load = pltpu.make_async_copy(out_weight, weight, sem2.at[late])
    weight_load.start()
    for load in loads:
        load.wait()
    final_refs = [last.at[i] for i in range(late)]
    for column in range(0, 2 * width, 256):
        columns = slice(column, column + 256)
        gathered = gkv[:, columns] + gather_global(
            pos[...], devs, arrays - late, final_refs, columns
        ).astype(BF16)
        keys[0, span:, columns] = gathered
        keys[1, span:, columns] = gathered
    placed[...] = jnp.zeros_like(placed)
    global_partial(count[0], gq, final_refs, scores, top2, sum2, acc2)

    def merge(tile, carry):
        at = pl.ds(pl.multiple_of(tile * TILE, TILE), TILE)
        top = jnp.maximum(top1[at, :], top2[at, :])
        one = jnp.exp2((top1[at, :] - top) * EXP2)
        two = jnp.exp2((top2[at, :] - top) * EXP2)
        total = sum1[at, :] * one + sum2[at, :] * two
        placed[at, :] = ((acc1[at, :] * one + acc2[at, :] * two) / total).astype(BF16)
        return carry

    lax.fori_loop(0, (count[0] + TILE - 1) // TILE, merge, 0)

    def one_block(block, carry):
        slot = lax.rem(block, 2)

        @pl.when(block + 1 < blocks)
        def _():
            copies(block + 1, 1 - slot, "start")

        copies(block, slot, "wait")
        at = pl.ds(pl.multiple_of(block * BLOCK, BLOCK), BLOCK)
        for group in range(width // GW):
            columns = slice(group * GW, (group + 1) * GW)
            values = slice(width + group * GW, width + (group + 1) * GW)
            left = spread_heads(queries[at, columns])
            score = contract_last(left, keys[slot, :, columns])
            top = jnp.max(score, axis=1, keepdims=True)
            probs = jnp.exp2((score - top) * EXP2)
            total = jnp.sum(probs, axis=1, keepdims=True)
            weighted = jnp.dot(
                probs.astype(BF16), keys[slot, :, values], preferred_element_type=F32
            )
            mixed[at, columns] = pick_heads(weighted / total, BLOCK).astype(BF16)
        return carry

    lax.fori_loop(0, blocks, one_block, 0)
    row = lax.broadcasted_iota(jnp.int32, (rows, NGLOB), 0)
    select = row == local_row[...]
    owned = jnp.max(select.astype(F32), axis=1, keepdims=True) > 0.5
    select = select.astype(BF16)
    for column in range(0, width, 256):
        columns = slice(column, column + 256)
        moved = jnp.dot(select, placed[:, columns], preferred_element_type=F32).astype(BF16)
        mixed[:, columns] = jnp.where(owned, moved, mixed[:, columns])
    weight_load.wait()
    for column in range(0, width, 256):
        columns = slice(column, column + 256)
        out[:, columns] = jnp.dot(
            mixed[...], weight[:, columns], preferred_element_type=F32
        ).astype(BF16)


def finish(late, devs, count, ids, offsets, pos, local_row, queries, state, out_weight, kv):
    rows, width = queries.shape
    keys = (3 + RAND) * BLOCK + NGLOB
    return pl.pallas_call(
        functools.partial(late_kernel, len(kv), late),
        out_shape=jax.ShapeDtypeStruct((rows, width), BF16),
        in_specs=[SMEM] * 4 + [VMEM] * 8 + [ANY] * (1 + len(kv)),
        out_specs=VMEM,
        scratch_shapes=[
            pltpu.VMEM((2, keys, 2 * width), BF16),
            pltpu.VMEM((width, width), BF16),
            pltpu.VMEM((late, rows, 2 * width), BF16),
            pltpu.VMEM((rows, width), BF16),
            pltpu.VMEM((NGLOB, width), F32),
            pltpu.VMEM((NGLOB, width), F32),
            pltpu.VMEM((NGLOB, width), F32),
            pltpu.VMEM((NGLOB, width), BF16),
            pltpu.VMEM((GROUP * TILE, late * rows), F32),
            pltpu.SemaphoreType.DMA((2, 3 + RAND)),
            pltpu.SemaphoreType.DMA((late + 1,)),
        ],
        compiler_params=params(48),
        name="finish",
    )(devs, count, ids, offsets, pos, local_row, queries, *state, out_weight, *kv)


def body(
    tokens,
    norm_gain,
    query_weight,
    key_weight,
    value_weight,
    out_weight,
    random_blocks,
    bucket_id,
    global_positions,
):
    shards = lax.axis_size("seq")
    device = lax.axis_index("seq").astype(jnp.int32)
    rows = tokens.shape[0]
    width = tokens.shape[1]
    local_blocks = rows // BLOCK
    half = rows // 2
    gain = norm_gain.reshape(1, width)
    pair = (key_weight, value_weight)

    kv = []
    owners = []
    if shards == 8:
        low, high = tokens[:half], tokens[half:]
        low2, high4 = exchange(low, 2), exchange(high, 4)
        high2, low4 = exchange(high, 2), exchange(low, 4)
        low6, high6 = exchange(low2, 4), exchange(high4, 2)
        own, queries = project([tokens], gain, (*pair, query_weight))
        rounds = [
            (own, 0, 0),
            (project([low2, high4], gain, pair)[0], 2, 4),
            (project([low4, high2], gain, pair)[0], 4, 2),
            (project([low6, high6], gain, pair)[0], 6, 6),
        ]
    else:
        have = {0: tokens}
        bit = 2
        while bit < shards:
            for j in list(have):
                have[j | bit] = exchange(have[j], bit)
            bit *= 2
        own, queries = project([tokens], gain, (*pair, query_weight))
        rounds = [(own, 0, 0)]
        for j in sorted(have)[1:]:
            rounds.append((project([have[j]], gain, pair)[0], j, j))
    for array, first, second in rounds:
        kv += [array, exchange(array, 1)]
        owners += [first, second, first ^ 1, second ^ 1]
    devs = device ^ jnp.array(owners, jnp.int32)

    block = device * local_blocks + jnp.arange(local_blocks, dtype=jnp.int32)
    total = shards * local_blocks
    window = jnp.stack([(block + total - 1) % total, block, (block + 1) % total], axis=1)
    mine = lax.dynamic_slice_in_dim(random_blocks, device * local_blocks, local_blocks, 0)
    chosen = jnp.concatenate([window, mine.astype(jnp.int32)], axis=1).reshape(-1)
    inner = chosen % local_blocks
    slot = (chosen // local_blocks) ^ device
    if shards == 8:
        upper = (inner >= local_blocks // 2).astype(jnp.int32)
        hop = slot >> 1
        step = jnp.where(hop == 1, 1 + upper, jnp.where(hop == 2, 2 - upper, hop))
        ids = 2 * step + (slot & 1)
    else:
        ids = slot
    offsets = inner * BLOCK

    positions = lax.dynamic_index_in_dim(global_positions, bucket_id[0], 0, False)
    positions = positions.astype(jnp.int32)
    local = positions - device * rows
    first = jnp.sum((local < 0).astype(jnp.int32))
    count = jnp.sum(((local >= 0) & (local < rows)).astype(jnp.int32)).reshape(1)
    padded = jnp.concatenate([local, jnp.full((NGLOB,), -1, jnp.int32)])
    compact = lax.dynamic_slice_in_dim(padded, first, NGLOB, 0)
    pos = positions.reshape(NGLOB, 1)

    state = early(devs, count, pos, compact.reshape(NGLOB, 1), queries, kv[:-2])
    return finish(
        2,
        devs,
        count,
        ids,
        offsets,
        pos,
        compact.reshape(1, NGLOB),
        queries,
        state,
        out_weight,
        kv,
    )


def solution(mesh):
    placed = (P(("dp", "seq"), None), P(), P(), P(), P(), P(), P("dp", None), P(), P())
    return jax.shard_map(
        body, mesh=mesh, in_specs=placed, out_specs=P(("dp", "seq"), None), check_vma=False
    )
```

time: 271 us -> 91.4 us (0.34)
  waiting for transfers between devices: 76.3 us -> 10.7 us
  local copies, waits for them, and re-layouts: 74.2 us -> 13.8 us
  Pallas kernels: 0 us -> 51.6 us
  matrix products: 46.6 us -> 0 us
  other arithmetic: 31.5 us -> 1.94 us
  blocking collectives: 17.6 us -> 0 us
  between operations: 14.4 us -> 2.7 us
    psum x1 -> x0, waiting for transfers between devices: 71 us -> none  [body(): lax.psum(jnp.dot(selector, normed, preferred_element_type=jnp.float32).as...]
    pallas_call x0 -> x6, Pallas kernels: none -> 51.6 us  [the longest x1 19.1 us: finish(): pl.pallas_call(functools.partial(late_kernel, len(kv), late), out_shape=j...]
    dot_general x11 -> x0, matrix products: 36.2 us -> none  [the longest x1 10.9 us: body(): jnp.einsum('bhqk,bkhd->bqhd', probs, value_part, preferred_element_type=j...]
    slice x11 -> x1, local copies, waits for them, and re-layouts: 34.8 us -> 1.36 us  [body(): low, high = (tokens[:half], tokens[half:])]
    all_gather x2 -> x0, blocking collectives: 17.6 us -> none  [combined_all(): pieces = jax.tree.map(lambda part: lax.all_gather(part, axis), value)]
    concatenate x4 -> x1, other arithmetic: 15.4 us -> 0.01 us  [body(): jnp.concatenate([window, mine.astype(jnp.int32)], axis=1).reshape(-1)]
    gather x2 -> x0, local copies, waits for them, and re-layouts: 13.4 us -> none  [the longest x1 7.37 us: body(): random_rows = incoming[my_source * capacity + my_rank]]
    sub x1 -> x0, matrix products: 10.5 us -> none  [body(): expo = jnp.exp(scores - top_score)]
  transfers between devices with their start and end apart: 5 -> 10, of which waited for: 3 -> 2; matrix products, arithmetic and copies ran while one was open for 38% -> 5% of each run, Pallas kernels for 0% -> 36%
where the time goes in v1:
time: 91.4 us; the launch traced here: 90.6 us
  Pallas kernels  51.6 us (56%)
  local copies, waits for them, and re-layouts  13.8 us (15%)
  waiting for transfers between devices  10.7 us (12%)
  starting transfers between devices  9.88 us (11%)
  between operations  2.7 us (3%)
  other arithmetic  1.94 us (2%)
    pallas_call x1, Pallas kernels, finish(): pl.pallas_call(functools.partial(late_kernel, len(kv), late), out_shape=j...  19.1 us
    pallas_call x4, Pallas kernels, project(): pl.pallas_call(functools.partial(project_kernel, len(pieces), count), out...  19 us
    pallas_call x1, Pallas kernels, early(): pl.pallas_call(functools.partial(early_kernel, len(kv)), out_shape=[jax.S...  13.4 us
    ppermute x10, waiting for transfers between devices, exchange(): return lax.ppermute(value, 'seq', [(i, i ^ shift) for i in range(count)])  10.7 us
    unnamed x40, local copies, waits for them, and re-layouts  9.94 us
    ppermute x10, starting transfers between devices, exchange(): return lax.ppermute(value, 'seq', [(i, i ^ shift) for i in range(count)])  9.88 us
  transfers between devices with their start and end apart: 10, of which 2 were waited for; matrix products, arithmetic and copies ran while one was open for 5% of the time, Pallas kernels for 36%

profile of v1, /device:TPU:0, one launch (start us, length us, event | category | flops | bytes accessed | tf_op | source)
XLA Modules:
  0.0 90.6 jit_solution(17776346538512693544)
XLA Ops:
  0.0 1.4 %fusion.9 = (bf16[256,1024]{1,0:T(8,128)(2,1)S(1)}, bf16[256,1024]{1,0:T(8,128)(2,1)S(1)}) fusion(bf16[512,1024]{1,0:T(8,128)(2,1)} %refs_0_.1), kind=kLoop, calls=%fused_computation.33 | loop fusion | bytes 2097152 | tf_op jit(solution)/shard_map/slice | solution.py:378
  1.4 3.0 %collective-permute-start.2 = (bf16[256,1024]{1,0:T(8,128)(2,1)S(1)}, bf16[256,1024]{1,0:T(8,128)(2,1)S(1)}, u32[]{:S(2)}, u32[]{:S(2)}) collective-permute-start(bf16[256,1024]{1,0:T(8,128)(2,1)S(1)} %get-tuple-element.22), channel_id=1, source_target_pairs={{0,16},{4,20},{8,24},{12,28},{16,0},{20,4},{24,8},{28,12},{1,17},{... | collective-permute-start | bytes 1572872 | tf_op jit(solution)/shard_map/ppermute | solution.py:33
  4.4 1.5 %collective-permute-start.1 = (bf16[256,1024]{1,0:T(8,128)(2,1)S(1)}, bf16[256,1024]{1,0:T(8,128)(2,1)S(1)}, u32[]{:S(2)}, u32[]{:S(2)}) collective-permute-start(bf16[256,1024]{1,0:T(8,128)(2,1)S(1)} %get-tuple-element.23), channel_id=1, source_target_pairs={{0,8},{4,12},{8,0},{12,4},{16,24},{20,28},{24,16},{28,20},{1,9},{5... | collective-permute-start | bytes 1572872 | tf_op jit(solution)/shard_map/ppermute | solution.py:33
  5.9 0.5 collective-permute-start.5
  6.5 10.6 %collective-permute-done.2.refs_1_ = bf16[256,1024]{1,0:T(8,128)(2,1)S(1)} collective-permute-done((bf16[256,1024]{1,0:T(8,128)(2,1)S(1)}, bf16[256,1024]{1,0:T(8,128)(2,1)S(1)}, u32[]{:S(2)}, u32[]{:S(2)}) %collective-permute-start.2) | collective-permute-done | bytes 524320 | tf_op jit(solution)/shard_map/ppermute | solution.py:33
  17.2 2.0 %collective-permute-start.8 = (bf16[256,1024]{1,0:T(8,128)(2,1)S(1)}, bf16[256,1024]{1,0:T(8,128)(2,1)S(1)}, u32[]{:S(2)}, u32[]{:S(2)}) collective-permute-start(bf16[256,1024]{1,0:T(8,128)(2,1)S(1)} %collective-permute-done.2.refs_1_), channel_id=1, source_target_pairs={{0,8},{4,12},{8,0},{12,4},{16,24},{20,28},{24,16},{28,20},{1,9},{5... | collective-permute-start | bytes 1572872 | tf_op jit(solution)/shard_map/ppermute | solution.py:33
  19.3 1.5 %collective-permute-start.7 = (bf16[256,1024]{1,0:T(8,128)(2,1)S(1)}, bf16[256,1024]{1,0:T(8,128)(2,1)S(1)}, u32[]{:S(2)}, u32[]{:S(2)}) collective-permute-start(bf16[256,1024]{1,0:T(8,128)(2,1)S(1)} %collective-permute-done.1.refs_0_), channel_id=1, source_target_pairs={{0,16},{4,20},{8,24},{12,28},{16,0},{20,4},{24,8},{28,12},{1,17},{... | collective-permute-start | bytes 1572872 | tf_op jit(solution)/shard_map/ppermute | solution.py:33
  20.7 1.6 %copy-done.13 = bf16[1024,1024]{1,0:T(8,128)(2,1)S(1)} copy-done((bf16[1024,1024]{1,0:T(8,128)(2,1)S(1)}, bf16[1024,1024]{1,0:T(8,128)(2,1)}, u32[]{:S(2)}) %copy-start.13) | copy-done | bytes 2097176
  22.3 1.6 %copy-done.14 = bf16[1024,1024]{1,0:T(8,128)(2,1)S(1)} copy-done((bf16[1024,1024]{1,0:T(8,128)(2,1)S(1)}, bf16[1024,1024]{1,0:T(8,128)(2,1)}, u32[]{:S(2)}) %copy-start.14) | copy-done | bytes 2097176
  23.9 1.6 %copy-done.16 = bf16[1024,1024]{1,0:T(8,128)(2,1)S(1)} copy-done((bf16[1024,1024]{1,0:T(8,128)(2,1)S(1)}, bf16[1024,1024]{1,0:T(8,128)(2,1)}, u32[]{:S(2)}) %copy-start.16) | copy-done | bytes 2097176
  25.5 5.3 %project.4 = (bf16[512,2048]{1,0:T(8,128)(2,1)S(1)}, bf16[512,1024]{1,0:T(8,128)(2,1)S(1)}) custom-call(bf16[512,1024]{1,0:T(8,128)(2,1)S(1)} %copy-done.5, f32[1,1024]{1,0:T(1,128)S(1)} %bitcast.15, bf16[1024,1024]{1,0:T(8,128)(2,1)S(1)} %copy-done.14, bf16[1024,1024]{1,0:T(8,128)(2,1)S(1)} %copy-done.16, bf16[1024,1024]{1,0:T(8,128)(2,1)S(1)} %copy-done.13), custom_call_target="tpu_custom_call" | custom-call | flops 3221225472 | bytes 10485760 | tf_op jit(solution)/shard_map/project/pallas_call | solution.py:88
  30.9 4.5 %project.5.refs_7_.refs_15_ = bf16[512,2048]{1,0:T(8,128)(2,1)} custom-call(bf16[256,1024]{1,0:T(8,128)(2,1)S(1)} %collective-permute-done.1.refs_0_, bf16[256,1024]{1,0:T(8,128)(2,1)S(1)} %collective-permute-done.2.refs_1_, f32[1,1024]{1,0:T(1,128)S(1)} %bitcast.16, bf16[1024,1024]{1,0:T(8,128)(2,1)S(1)} %copy-done.15, bf16[1024,1024]{1,0:T(8,128)(2,1)S(1)} %copy-done.17), custom_call_target="tpu_custom_call" | custom-call | flops 2147483648 | bytes 7340032 | tf_op jit(solution)/shard_map/project/pallas_call | solution.py:88
  35.5 0.5 collective-permute-start.3
  36.0 4.6 %project.6.refs_9_.refs_17_ = bf16[512,2048]{1,0:T(8,128)(2,1)} custom-call(bf16[256,1024]{1,0:T(8,128)(2,1)S(1)} %collective-permute-done.4.refs_0_, bf16[256,1024]{1,0:T(8,128)(2,1)S(1)} %collective-permute-done.5.refs_1_, f32[1,1024]{1,0:T(1,128)S(1)} %bitcast.17, bf16[1024,1024]{1,0:T(8,128)(2,1)S(1)} %copy-done.15, bf16[1024,1024]{1,0:T(8,128)(2,1)S(1)} %copy-done.17), custom_call_target="tpu_custom_call" | custom-call | flops 2147483648 | bytes 7340032 | tf_op jit(solution)/shard_map/project/pallas_call | solution.py:88
  40.6 0.1 collective-permute-start.6
  40.7 4.7 %project.7.refs_19_ = bf16[512,2048]{1,0:T(8,128)(2,1)} custom-call(bf16[256,1024]{1,0:T(8,128)(2,1)S(1)} %collective-permute-done.7.refs_0_, bf16[256,1024]{1,0:T(8,128)(2,1)S(1)} %collective-permute-done.8.refs_1_, f32[1,1024]{1,0:T(1,128)S(1)} %bitcast.18, bf16[1024,1024]{1,0:T(8,128)(2,1)S(1)} %copy-done.15, bf16[1024,1024]{1,0:T(8,128)(2,1)S(1)} %copy-done.17), custom_call_target="tpu_custom_call" | custom-call | flops 2147483648 | bytes 7340032 | tf_op jit(solution)/shard_map/project/pallas_call | solution.py:88
  45.4 0.5 collective-permute-start.9
  46.6 1.3 %fusion.3 = (s32[]{:T(128)}, s32[]{:T(128)}, s32[128]{0:T(128)S(1)}) fusion(s32[]{:T(128)S(6)} %mul.16, s32[8,128]{1,0:T(8,128)} %param.18, s32[]{:T(128)S(6)} %select_n.52), kind=kLoop, calls=%fused_computation.21 | loop fusion | flops 1150 | bytes 1040 | tf_op jit(solution)/shard_map/reduce_sum | solution.py:424
  49.1 0.1 copy.11
  49.2 0.1 reshape.103
  49.3 0.7 fusion.6
  50.0 0.7 copy.14.refs_2_.refs_4_
  51.3 0.1 fusion.7
  51.4 0.7 copy.13.refs_3_
  52.1 0.5 broadcast_xor_fusion.refs_0_
  52.7 13.4 %early.1 = (bf16[128,1024]{1,0:T(8,128)(2,1)}, bf16[128,2048]{1,0:T(8,128)(2,1)}, f32[128,1024]{1,0:T(8,128)}, f32[128,1024]{1,0:T(8,128)}, f32[128,1024]{1,0:T(8,128)}) custom-call(s32[16]{0:T(128)} %broadcast_xor_fusion.refs_0_, s32[1]{0:T(128)} %bitcast.2.refs_1_, s32[128,1]{1,0:T(8,128)} %copy.14.refs_2_.refs_4_, s32[128,1]{1,0:T(8,128)} %copy.13.refs_3_, ...), custom_call_target="tpu_custom_call" | custom-call | flops 1610612736 | bytes 12582912 | tf_op jit(solution)/shard_map/early/pallas_call | solution.py:204
  66.2 1.0 %copy-done.7 = bf16[128,2048]{1,0:T(8,128)(2,1)S(1)} copy-done((bf16[128,2048]{1,0:T(8,128)(2,1)S(1)}, bf16[128,2048]{1,0:T(8,128)(2,1)}, u32[]{:S(2)}) %copy-start.7) | copy-done | bytes 524312
  67.2 1.0 %copy-done.8 = f32[128,1024]{1,0:T(8,128)S(1)} copy-done((f32[128,1024]{1,0:T(8,128)S(1)}, f32[128,1024]{1,0:T(8,128)}, u32[]{:S(2)}) %copy-start.8) | copy-done | bytes 524312
  68.3 1.0 %copy-done.9 = f32[128,1024]{1,0:T(8,128)S(1)} copy-done((f32[128,1024]{1,0:T(8,128)S(1)}, f32[128,1024]{1,0:T(8,128)}, u32[]{:S(2)}) %copy-start.9) | copy-done | bytes 524312
  69.3 1.0 %copy-done.10 = f32[128,1024]{1,0:T(8,128)S(1)} copy-done((f32[128,1024]{1,0:T(8,128)S(1)}, f32[128,1024]{1,0:T(8,128)}, u32[]{:S(2)}) %copy-start.10) | copy-done | bytes 524312
  70.4 0.9 %copy-done.11 = bf16[128,1024]{1,0:T(8,128)(2,1)S(1)} copy-done((bf16[128,1024]{1,0:T(8,128)(2,1)S(1)}, bf16[128,1024]{1,0:T(8,128)(2,1)}, u32[]{:S(2)}) %copy-start.11) | copy-done | bytes 262168
  71.3 19.1 %finish.1 = bf16[512,1024]{1,0:T(8,128)(2,1)} custom-call(s32[16]{0:T(128)S(1)} %copy-done.12, s32[1]{0:T(128)} %bitcast.2.refs_1_, s32[48]{0:T(128)S(1)} %get-tuple-element.27.refs_2_, s32[48]{0:T(128)S(1)} %get-tuple-element.26.refs_3_, s32[128,1]{1,0:T(8,128)S(1)} %copy-done.6, s32[1,128]{1,0:T(1,128)S(1)} %get-tuple-element.25.refs_5_, ...), custom_call_target="tpu_custom_call" | custom-call | tf_op jit(solution)/shard_map/finish/pallas_call | solution.py:332
  (48 shorter events, 0.4 us)
Async XLA Ops:
  0.0 49.0 %copy-start = (s32[64,3]{0,1:T(4,128)S(1)}, s32[64,3]{0,1:T(4,128)}, u32[]{:S(2)}) copy-start(s32[64,3]{0,1:T(4,128)} %param.16) | copy-start | bytes 2308
  0.0 20.7 %copy-start.5 = (bf16[512,1024]{1,0:T(8,128)(2,1)S(1)}, bf16[512,1024]{1,0:T(8,128)(2,1)}, u32[]{:S(2)}) copy-start(bf16[512,1024]{1,0:T(8,128)(2,1)} %refs_0_.1) | copy-start | bytes 3145732
  0.0 20.7 %copy-start.18 = (f32[1024]{0:T(1024)S(1)}, f32[1024]{0:T(1024)}, u32[]{:S(2)}) copy-start(f32[1024]{0:T(1024)} %param.11) | copy-start | bytes 12292
  1.4 15.8 %collective-permute-start.2 = (bf16[256,1024]{1,0:T(8,128)(2,1)S(1)}, bf16[256,1024]{1,0:T(8,128)(2,1)S(1)}, u32[]{:S(2)}, u32[]{:S(2)}) collective-permute-start(bf16[256,1024]{1,0:T(8,128)(2,1)S(1)} %get-tuple-element.22), channel_id=1, source_target_pairs={{0,16},{4,20},{8,24},{12,28},{16,0},{20,4},{24,8},{28,12},{1,17},{... | collective-permute-start | bytes 1572872 | tf_op jit(solution)/shard_map/ppermute | solution.py:33
  4.4 14.8 %collective-permute-start.1 = (bf16[256,1024]{1,0:T(8,128)(2,1)S(1)}, bf16[256,1024]{1,0:T(8,128)(2,1)S(1)}, u32[]{:S(2)}, u32[]{:S(2)}) collective-permute-start(bf16[256,1024]{1,0:T(8,128)(2,1)S(1)} %get-tuple-element.23), channel_id=1, source_target_pairs={{0,8},{4,12},{8,0},{12,4},{16,24},{20,28},{24,16},{28,20},{1,9},{5... | collective-permute-start | bytes 1572872 | tf_op jit(solution)/shard_map/ppermute | solution.py:33
  5.9 29.6 %collective-permute-start.5 = (bf16[256,1024]{1,0:T(8,128)(2,1)S(1)}, bf16[256,1024]{1,0:T(8,128)(2,1)S(1)}, u32[]{:S(2)}, u32[]{:S(2)}) collective-permute-start(bf16[256,1024]{1,0:T(8,128)(2,1)S(1)} %get-tuple-element.22), channel_id=1, source_target_pairs={{0,8},{4,12},{8,0},{12,4},{16,24},{20,28},{24,16},{28,20},{1,9},{5... | collective-permute-start | bytes 1572872 | tf_op jit(solution)/shard_map/ppermute | solution.py:33
  6.4 29.6 %collective-permute-start.4 = (bf16[256,1024]{1,0:T(8,128)(2,1)S(1)}, bf16[256,1024]{1,0:T(8,128)(2,1)S(1)}, u32[]{:S(2)}, u32[]{:S(2)}) collective-permute-start(bf16[256,1024]{1,0:T(8,128)(2,1)S(1)} %get-tuple-element.23), channel_id=1, source_target_pairs={{0,16},{4,20},{8,24},{12,28},{16,0},{20,4},{24,8},{28,12},{1,17},{... | collective-permute-start | bytes 1572872 | tf_op jit(solution)/shard_map/ppermute | solution.py:33
  17.2 23.5 %collective-permute-start.8 = (bf16[256,1024]{1,0:T(8,128)(2,1)S(1)}, bf16[256,1024]{1,0:T(8,128)(2,1)S(1)}, u32[]{:S(2)}, u32[]{:S(2)}) collective-permute-start(bf16[256,1024]{1,0:T(8,128)(2,1)S(1)} %collective-permute-done.2.refs_1_), channel_id=1, source_target_pairs={{0,8},{4,12},{8,0},{12,4},{16,24},{20,28},{24,16},{28,20},{1,9},{5... | collective-permute-start | bytes 1572872 | tf_op jit(solution)/shard_map/ppermute | solution.py:33
  19.3 21.4 %collective-permute-start.7 = (bf16[256,1024]{1,0:T(8,128)(2,1)S(1)}, bf16[256,1024]{1,0:T(8,128)(2,1)S(1)}, u32[]{:S(2)}, u32[]{:S(2)}) collective-permute-start(bf16[256,1024]{1,0:T(8,128)(2,1)S(1)} %collective-permute-done.1.refs_0_), channel_id=1, source_target_pairs={{0,16},{4,20},{8,24},{12,28},{16,0},{20,4},{24,8},{28,12},{1,17},{... | collective-permute-start | bytes 1572872 | tf_op jit(solution)/shard_map/ppermute | solution.py:33
  20.7 1.6 %copy-start.13 = (bf16[1024,1024]{1,0:T(8,128)(2,1)S(1)}, bf16[1024,1024]{1,0:T(8,128)(2,1)}, u32[]{:S(2)}) copy-start(bf16[1024,1024]{1,0:T(8,128)(2,1)} %refs_4_.4) | copy-start | bytes 6291460
  22.3 1.6 %copy-start.14 = (bf16[1024,1024]{1,0:T(8,128)(2,1)S(1)}, bf16[1024,1024]{1,0:T(8,128)(2,1)}, u32[]{:S(2)}) copy-start(bf16[1024,1024]{1,0:T(8,128)(2,1)} %refs_3_.7) | copy-start | bytes 6291460
  23.9 1.6 %copy-start.16 = (bf16[1024,1024]{1,0:T(8,128)(2,1)S(1)}, bf16[1024,1024]{1,0:T(8,128)(2,1)}, u32[]{:S(2)}) copy-start(bf16[1024,1024]{1,0:T(8,128)(2,1)} %refs_4_.7) | copy-start | bytes 6291460
  25.5 5.4 %copy-start.15 = (bf16[1024,1024]{1,0:T(8,128)(2,1)S(1)}, bf16[1024,1024]{1,0:T(8,128)(2,1)}, u32[]{:S(2)}) copy-start(bf16[1024,1024]{1,0:T(8,128)(2,1)} %refs_3_.7) | copy-start | bytes 6291460
  25.5 5.4 %copy-start.17 = (bf16[1024,1024]{1,0:T(8,128)(2,1)S(1)}, bf16[1024,1024]{1,0:T(8,128)(2,1)}, u32[]{:S(2)}) copy-start(bf16[1024,1024]{1,0:T(8,128)(2,1)} %refs_4_.7) | copy-start | bytes 6291460
  30.8 4.7 %copy-start.1 = (bf16[512,2048]{1,0:T(8,128)(2,1)}, bf16[512,2048]{1,0:T(8,128)(2,1)S(1)}, u32[]{:S(2)}) copy-start(bf16[512,2048]{1,0:T(8,128)(2,1)S(1)} %get-tuple-element.13.refs_5_.refs_13_) | copy-start | bytes 6291460
  30.8 4.7 %copy-start.2 = (bf16[512,1024]{1,0:T(8,128)(2,1)}, bf16[512,1024]{1,0:T(8,128)(2,1)S(1)}, u32[]{:S(2)}) copy-start(bf16[512,1024]{1,0:T(8,128)(2,1)S(1)} %get-tuple-element.12.refs_4_.refs_6_) | copy-start | bytes 3145732
  30.8 21.9 %collective-permute-start = (bf16[512,2048]{1,0:T(8,128)(2,1)S(1)}, bf16[512,2048]{1,0:T(8,128)(2,1)}, u32[]{:S(2)}, u32[]{:S(2)}) collective-permute-start(bf16[512,2048]{1,0:T(8,128)(2,1)S(1)} %get-tuple-element.13.refs_5_.refs_13_), channel_id=1, source_target_pairs={{0,4},{4,0},{8,12},{12,8},{16,20},{20,16},{24,28},{28,24},{1,5},{5... | collective-permute-start | bytes 6291464 | tf_op jit(solution)/shard_map/ppermute | solution.py:33
  35.5 17.2 %collective-permute-start.3 = (bf16[512,2048]{1,0:T(8,128)(2,1)}, bf16[512,2048]{1,0:T(8,128)(2,1)}, u32[]{:S(2)}, u32[]{:S(2)}) collective-permute-start(bf16[512,2048]{1,0:T(8,128)(2,1)} %project.5.refs_7_.refs_15_), channel_id=1, source_target_pairs={{0,4},{4,0},{8,12},{12,8},{16,20},{20,16},{24,28},{28,24},{1,5},{5... | collective-permute-start | bytes 6291464 | tf_op jit(solution)/shard_map/ppermute | solution.py:33
  40.6 11.5 %copy-start.19 = (s32[16]{0:T(128)S(1)}, s32[16]{0:T(128)}, u32[]{:S(2)}) copy-start(s32[16]{0:T(128)} %constant.77.clone) | copy-start | bytes 196
  40.6 12.1 %collective-permute-start.6 = (bf16[512,2048]{1,0:T(8,128)(2,1)}, bf16[512,2048]{1,0:T(8,128)(2,1)}, u32[]{:S(2)}, u32[]{:S(2)}) collective-permute-start(bf16[512,2048]{1,0:T(8,128)(2,1)} %project.6.refs_9_.refs_17_), channel_id=1, source_target_pairs={{0,4},{4,0},{8,12},{12,8},{16,20},{20,16},{24,28},{28,24},{1,5},{5... | collective-permute-start | bytes 6291464 | tf_op jit(solution)/shard_map/ppermute | solution.py:33
  45.4 20.8 %collective-permute-start.9 = (bf16[512,2048]{1,0:T(8,128)(2,1)}, bf16[512,2048]{1,0:T(8,128)(2,1)}, u32[]{:S(2)}, u32[]{:S(2)}) collective-permute-start(bf16[512,2048]{1,0:T(8,128)(2,1)} %project.7.refs_19_), channel_id=1, source_target_pairs={{0,4},{4,0},{8,12},{12,8},{16,20},{20,16},{24,28},{28,24},{1,5},{5... | collective-permute-start | bytes 6291464 | tf_op jit(solution)/shard_map/ppermute | solution.py:33
  52.7 13.5 %copy-start.3 = (bf16[512,1024]{1,0:T(8,128)(2,1)S(1)}, bf16[512,1024]{1,0:T(8,128)(2,1)}, u32[]{:S(2)}) copy-start(bf16[512,1024]{1,0:T(8,128)(2,1)} %copy-done.2) | copy-start | bytes 3145732
  52.7 13.5 %copy-start.4 = (bf16[1024,1024]{1,0:T(8,128)(2,1)S(1)}, bf16[1024,1024]{1,0:T(8,128)(2,1)}, u32[]{:S(2)}) copy-start(bf16[1024,1024]{1,0:T(8,128)(2,1)} %refs_12_.1) | copy-start | bytes 6291460
  52.7 13.5 %copy-start.6 = (s32[128,1]{1,0:T(8,128)S(1)}, s32[128,1]{1,0:T(8,128)}, u32[]{:S(2)}) copy-start(s32[128,1]{1,0:T(8,128)} %copy.14.refs_2_.refs_4_) | copy-start | bytes 1540
  52.7 13.5 %copy-start.12 = (s32[16]{0:T(128)S(1)}, s32[16]{0:T(128)}, u32[]{:S(2)}) copy-start(s32[16]{0:T(128)} %broadcast_xor_fusion.refs_0_) | copy-start | bytes 196
  66.2 1.0 %copy-start.7 = (bf16[128,2048]{1,0:T(8,128)(2,1)S(1)}, bf16[128,2048]{1,0:T(8,128)(2,1)}, u32[]{:S(2)}) copy-start(bf16[128,2048]{1,0:T(8,128)(2,1)} %get-tuple-element.15.refs_8_) | copy-start | bytes 1572868
  67.2 1.0 %copy-start.8 = (f32[128,1024]{1,0:T(8,128)S(1)}, f32[128,1024]{1,0:T(8,128)}, u32[]{:S(2)}) copy-start(f32[128,1024]{1,0:T(8,128)} %get-tuple-element.16.refs_9_) | copy-start | bytes 1572868
  68.3 1.0 %copy-start.9 = (f32[128,1024]{1,0:T(8,128)S(1)}, f32[128,1024]{1,0:T(8,128)}, u32[]{:S(2)}) copy-start(f32[128,1024]{1,0:T(8,128)} %get-tuple-element.17.refs_10_) | copy-start | bytes 1572868
  69.3 1.0 %copy-start.10 = (f32[128,1024]{1,0:T(8,128)S(1)}, f32[128,1024]{1,0:T(8,128)}, u32[]{:S(2)}) copy-start(f32[128,1024]{1,0:T(8,128)} %get-tuple-element.18.refs_11_) | copy-start | bytes 1572868
  70.4 0.9 %copy-start.11 = (bf16[128,1024]{1,0:T(8,128)(2,1)S(1)}, bf16[128,1024]{1,0:T(8,128)(2,1)}, u32[]{:S(2)}) copy-start(bf16[128,1024]{1,0:T(8,128)(2,1)} %get-tuple-element.14.refs_7_) | copy-start | bytes 786436

commit v2 on v0

v2 whole, which is shorter than its diff:
```python
import functools
import math

import jax
import jax.numpy as jnp
from jax import lax
from jax.experimental import pallas as pl
from jax.experimental.pallas import tpu as pltpu
from jax.sharding import PartitionSpec as P

HEADS = 16
HDIM = 64
BLOCK = 64
RAND = 3
NGLOB = 128
GROUP = 4
GW = GROUP * HDIM
TILE = 32
PICKS = 3 + RAND
EXP2 = HDIM ** (-0.5) * math.log2(math.e)
F32 = jnp.float32
BF16 = jnp.bfloat16
HBM = pl.BlockSpec(memory_space=pltpu.HBM)
VMEM = pl.BlockSpec(memory_space=pltpu.VMEM)
SMEM = pl.BlockSpec(memory_space=pltpu.SMEM)
COST = pl.CostEstimate(flops=1024, bytes_accessed=1024, transcendentals=0)


def params(mib):
    return pltpu.CompilerParams(vmem_limit_bytes=mib << 20)


LIMIT = 60


def hops_of(shards):
    if shards == 8:
        return [(0, 0), (2, 4), (4, 2), (6, 6)]
    return [(2 * step, 2 * step) for step in range(shards // 2)]


def layer_norm(tokens, gain):
    values = tokens.astype(F32)
    center = values - jnp.mean(values, axis=-1, keepdims=True)
    spread = jnp.mean(center * center, axis=-1, keepdims=True)
    return (center * lax.rsqrt(spread + 1e-05) * gain).astype(BF16)


def head_lane(rows):
    return lax.broadcasted_iota(jnp.int32, (rows, GW), 1) // HDIM


def spread_heads(rows):
    lane = head_lane(rows.shape[0])
    masks = [(lane == head).astype(BF16) for head in range(GROUP)]
    return jnp.concatenate([rows * mask for mask in masks], axis=0)


def pick_heads(stacked, rows):
    lane = head_lane(rows)
    picked = stacked[(GROUP - 1) * rows :]
    for head in range(GROUP - 1):
        picked = jnp.where(lane == head, stacked[head * rows : (head + 1) * rows], picked)
    return picked


def contract_last(left, right):
    return lax.dot_general(left, right, (((1,), (1,)), ((), ())), preferred_element_type=F32)


def square(axis):
    return lax.broadcasted_iota(jnp.int32, (NGLOB, NGLOB), axis)


class Globals:
    def __init__(self, bucket, table, rows):
        self.me = lax.axis_index("seq")
        self.rows = rows
        self.row = table[pl.ds(bucket[0], 1), :]
        self.local = self.row - self.me * rows
        self.first = jnp.sum((self.local < 0).astype(F32)).astype(jnp.int32)
        below = jnp.sum((self.local < rows).astype(F32)).astype(jnp.int32)
        self.count = below - self.first
        self.tiles = (self.count + TILE - 1) // TILE

    def column(self):
        spread = jnp.where(square(0) == square(1), self.row, 0).astype(F32)
        return jnp.sum(spread, axis=1, keepdims=True).astype(jnp.int32)

    def own_column(self):
        hit = jnp.where(square(1) == square(0) + self.first, self.local, 0).astype(F32)
        found = jnp.sum(hit, axis=1, keepdims=True).astype(jnp.int32)
        index = lax.broadcasted_iota(jnp.int32, (NGLOB, 1), 0)
        return jnp.where(index < self.count, found, -1)

    def own_row(self):
        local = self.column() - self.me * self.rows
        hit = jnp.where(square(0) == square(1) + self.first, local, 0).astype(F32)
        found = jnp.sum(hit, axis=0, keepdims=True).astype(jnp.int32)
        index = lax.broadcasted_iota(jnp.int32, (1, NGLOB), 1)
        return jnp.where(index < self.count, found, -1)


def owner(me, step, core, shards):
    even, odd = hops_of(shards)[step]
    there = me ^ core
    return there ^ jnp.where(there & 1 == 0, even, odd)


def place_of(device, me, shards):
    slot = device ^ me
    core = slot & 1
    hop = slot - core
    if shards != 8:
        return hop // 2, core
    parity = (me ^ core) & 1
    near = jnp.where((hop == 2) == (parity == 0), 1, 2)
    return jnp.where(hop == 0, 0, jnp.where(hop == 6, 3, near)), core


def start_loads(sources, targets, sems):
    loads = []
    for index, (source, target) in enumerate(zip(sources, targets)):
        load = pltpu.make_async_copy(source, target, sems.at[index])
        load.start()
        loads.append(load)
    return loads


def normalize(loads, tokens, gain, normed, info, bases):
    pieces, rows, width = tokens.shape
    total = pieces * rows
    for piece in range(pieces):
        loads[piece].wait()
        for start in range(0, rows, 128):
            at = piece * rows + start
            normed[at : at + 128, :] = layer_norm(tokens[piece, start : start + 128, :], gain[...])
    lane = lax.broadcasted_iota(jnp.int32, (1, total), 1)
    column = info.column()
    where = jnp.full((NGLOB, 1), -1, jnp.int32)
    for piece, base in enumerate(bases):
        inside = column - base * rows
        hit = jnp.where(inside < 0, rows, inside) < rows
        where = jnp.where(hit, inside + piece * rows, where)
    select = (where == lane).astype(BF16)
    for start in range(0, width, 256):
        columns = slice(start, start + 256)
        normed[total:, columns] = jnp.dot(
            select, normed[:total, columns], preferred_element_type=F32
        ).astype(BF16)


def multiply(normed, weight, results, offset):
    for start in range(0, weight.shape[1], 256):
        results[:, offset + start : offset + start + 256] = jnp.dot(
            normed[...], weight[:, start : start + 256], preferred_element_type=F32
        ).astype(BF16)


def global_partial(tiles, gq, kv, total, scores, state):
    width = gq.shape[1]

    def one_tile(tile, carry):
        at = pl.ds(pl.multiple_of(tile * TILE, TILE), TILE)
        for group in range(width // GW):
            columns = slice(group * GW, (group + 1) * GW)
            values = slice(width + group * GW, width + (group + 1) * GW)
            left = spread_heads(gq[at, columns])
            scores[...] = contract_last(left, kv[:total, columns])
            top = jnp.max(scores[...], axis=1, keepdims=True)
            probs = jnp.exp2((scores[...] - top) * EXP2)
            part = jnp.sum(probs, axis=1, keepdims=True)
            acc = jnp.dot(probs.astype(BF16), kv[:total, values], preferred_element_type=F32)
            shape = (GROUP * TILE, GW)
            for index, value in enumerate(
                (jnp.broadcast_to(top, shape), jnp.broadcast_to(part, shape), acc)
            ):
                state[index, at, columns] = pick_heads(value, TILE)
        return carry

    lax.fori_loop(0, tiles, one_tile, 0)


def move_state(tiles, pairs, sems, act):
    for tile in range(NGLOB // TILE):

        @pl.when(tile < tiles)
        def _():
            rows = slice(tile * TILE, (tile + 1) * TILE)
            for index, (source, target) in enumerate(pairs):
                copy = pltpu.make_async_copy(
                    source.at[:, rows, :], target.at[:, rows, :], sems.at[tile, index]
                )
                copy.start() if act == "start" else copy.wait()


def merge_states(tiles, states, target):
    def one_tile(tile, carry):
        at = pl.ds(pl.multiple_of(tile * TILE, TILE), TILE)
        top = functools.reduce(jnp.maximum, [ref[0, at, :] for ref in states])
        total = jnp.zeros_like(top)
        acc = jnp.zeros_like(top)
        for ref in states:
            factor = jnp.exp2((ref[0, at, :] - top) * EXP2)
            total += ref[1, at, :] * factor
            acc += ref[2, at, :] * factor
        target[at, :] = (acc / total).astype(BF16)
        return carry

    lax.fori_loop(0, tiles, one_tile, 0)


def rows_kernel(shards, places, *refs):
    count = len(places)
    first = places[0][0] == 0
    bucket, table, gain = refs[:3]
    sources = refs[3 : 3 + count]
    weights = refs[3 + count : 5 + count + first]
    at = 5 + count + first
    if first:
        out, gsum, kept, queries, gq = refs[at : at + 5]
        at += 5
    else:
        gq, gold, out, gsum, kept = refs[at : at + 5]
        at += 5
    tokens, weight, normed, results, state, scores, token_sems, weight_sems, out_sems, sems = refs[
        at : at + 10
    ]
    rows, width = sources[0].shape
    total = count * rows
    loads = start_loads(sources, [tokens.at[i] for i in range(count)], token_sems)
    order = [2, 0, 1] if first else [0, 1]
    arrivals = start_loads(
        [weights[i] for i in order], [weight.at[i] for i in order], weight_sems
    )
    info = Globals(bucket, table, rows)
    bases = [owner(info.me, step, core, shards) for step, core in places]
    normalize(loads, tokens, gain, normed, info, bases)
    if first:
        arrivals.pop(0).wait()
        lane = lax.broadcasted_iota(jnp.int32, (1, rows), 1)
        select = (info.own_column() == lane).astype(BF16)
        for start in range(0, width, 256):
            columns = slice(start, start + 256)
            query = jnp.dot(
                normed[:rows, :], weight[2, :, columns], preferred_element_type=F32
            ).astype(BF16)
            queries[:, columns] = query
            gq[:, columns] = jnp.dot(select, query, preferred_element_type=F32).astype(BF16)
    stores = []
    for index in range(2):
        arrivals[index].wait()
        multiply(normed, weight.at[index], results, index * width)
        columns = slice(index * width, (index + 1) * width)
        store = pltpu.make_async_copy(
            results.at[:total, columns], out.at[:, columns], out_sems.at[index]
        )
        store.start()
        stores.append(store)
    gsum[...] = results[total:, :] if first else gold[...] + results[total:, :]
    global_partial(info.tiles, gq, results, total, scores, state)
    move_state(info.tiles, [(state, kept)], sems, "start")
    move_state(info.tiles, [(state, kept)], sems, "wait")
    for store in stores:
        store.wait()


def call(kernel, inputs, specs, outs, out_specs, scratch, name):
    return pl.pallas_call(
        kernel,
        out_shape=[jax.ShapeDtypeStruct(*out) for out in outs],
        in_specs=specs,
        out_specs=out_specs,
        scratch_shapes=scratch,
        compiler_params=params(LIMIT),
        cost_estimate=COST,
        name=name,
    )(*inputs)


def project_scratch(count, rows, width, weights):
    total = count * rows + NGLOB
    return [
        pltpu.VMEM((count, rows, width), BF16),
        pltpu.VMEM((weights, width, width), BF16),
        pltpu.VMEM((total, width), BF16),
        pltpu.VMEM((total, 2 * width), BF16),
        pltpu.VMEM((3, NGLOB, width), F32),
        pltpu.VMEM((GROUP * TILE, count * rows), F32),
        pltpu.SemaphoreType.DMA((count,)),
        pltpu.SemaphoreType.DMA((weights,)),
    ]


def rows_call(shards, places, index, gain, pieces, weights, *chain):
    rows, width = pieces[0].shape
    first = places[0][0] == 0
    outs = [
        ((len(pieces) * rows, 2 * width), BF16),
        ((NGLOB, 2 * width), BF16),
        ((3, NGLOB, width), F32),
    ]
    if first:
        outs += [((rows, width), BF16), ((NGLOB, width), BF16)]
    return call(
        functools.partial(rows_kernel, shards, places),
        [*index, gain, *pieces, *weights, *chain],
        [SMEM, VMEM, VMEM] + [HBM] * (len(pieces) + len(weights)) + [VMEM] * len(chain),
        outs,
        [HBM, VMEM, HBM] + [VMEM] * (2 * first),
        project_scratch(len(pieces), rows, width, len(weights))
        + [pltpu.SemaphoreType.DMA((2,)), pltpu.SemaphoreType.DMA((NGLOB // TILE, 1))],
        "first" if first else "middle",
    )


def last_kernel(shards, parts, places, *refs):
    bucket, table, blocks_ref, gain, gq, gold, queries = refs[:7]
    sources = refs[7:9]
    weights = refs[9:12]
    part_refs = refs[12 : 12 + parts]
    kv_refs = refs[12 + parts : 12 + 2 * parts]
    out = refs[12 + 2 * parts]
    tokens, weight, normed, results, state, scores, token_sems, weight_sems = refs[
        13 + 2 * parts : 21 + 2 * parts
    ]
    keys, mixed, placed, olds, sems, state_sems = refs[21 + 2 * parts :]
    rows, width = queries.shape
    total = 2 * rows
    blocks = rows // BLOCK
    span = PICKS * BLOCK
    total_blocks = shards * blocks
    steps = shards // 2
    loads = start_loads(sources, [tokens.at[i] for i in range(2)], token_sems)
    arrivals = start_loads(weights, [weight.at[i] for i in range(3)], weight_sems)
    info = Globals(bucket, table, rows)
    me = info.me
    olds_refs = [olds.at[i] for i in range(parts)]
    pairs = list(zip(part_refs, olds_refs))
    move_state(info.tiles, pairs, state_sems, "start")

    def copies(block, slot, act):
        for pick in range(PICKS):
            target = keys.at[slot, pl.ds(pick * BLOCK, BLOCK), :]
            sem = sems.at[slot, pick]
            if act == "wait":
                pltpu.make_async_copy(kv_refs[0].at[pl.ds(0, BLOCK), :], target, sem).wait()
                continue
            here = me * blocks + block
            if pick < 3:
                chosen = lax.rem(here + total_blocks + pick - 1, total_blocks)
            else:
                chosen = blocks_ref[here, pick - 3]
            device = chosen // blocks
            step, core = place_of(device, me, shards)
            flat = jnp.where(step == 0, core, 2 * step - 2 + core)
            late = step == steps - 1
            piece = jnp.where(late, core, flat % 4)
            source = jnp.where(step == 0, 0, jnp.where(late, parts, 1 + flat // 4))
            start = piece * rows + (chosen - device * blocks) * BLOCK
            start = pl.multiple_of(start, BLOCK)
            for index in range(parts + 1):
                held = results if index == parts else kv_refs[index]

                @pl.when(source == index)
                def _():
                    pltpu.make_async_copy(held.at[pl.ds(start, BLOCK), :], target, sem).start()

    bases = [owner(me, step, core, shards) for step, core in places]
    normalize(loads, tokens, gain, normed, info, bases)
    for index in range(2):
        arrivals[index].wait()
        multiply(normed, weight.at[index], results, index * width)
    copies(0, 0, "start")
    gathered = gold[...] + results[total:, :]
    keys[0, span:, :] = gathered
    keys[1, span:, :] = gathered
    placed[...] = jnp.zeros_like(placed)
    global_partial(info.tiles, gq, results, total, scores, state)
    move_state(info.tiles, pairs, state_sems, "wait")
    merge_states(info.tiles, [state, *olds_refs], placed)

    def one_block(block, carry):
        slot = lax.rem(block, 2)

        @pl.when(block + 1 < blocks)
        def _():
            copies(block + 1, 1 - slot, "start")

        copies(block, slot, "wait")
        at = pl.ds(pl.multiple_of(block * BLOCK, BLOCK), BLOCK)
        groups = range(width // GW)
        score = [
            contract_last(
                spread_heads(queries[at, g * GW : (g + 1) * GW]),
                keys[slot, :, g * GW : (g + 1) * GW],
            )
            for g in groups
        ]
        probs = []
        totals = []
        for g in groups:
            top = jnp.max(score[g], axis=1, keepdims=True)
            prob = jnp.exp2((score[g] - top) * EXP2)
            totals.append(jnp.sum(prob, axis=1, keepdims=True))
            probs.append(prob.astype(BF16))
        for g in groups:
            weighted = jnp.dot(
                probs[g],
                keys[slot, :, width + g * GW : width + (g + 1) * GW],
                preferred_element_type=F32,
            )
            mixed[at, g * GW : (g + 1) * GW] = pick_heads(
                weighted * (1.0 / totals[g]), BLOCK
            ).astype(BF16)
        return carry

    lax.fori_loop(0, blocks, one_block, 0)
    row = lax.broadcasted_iota(jnp.int32, (rows, NGLOB), 0)
    select = row == info.own_row()
    owned = jnp.max(select.astype(F32), axis=1, keepdims=True) > 0.5
    select = select.astype(BF16)
    for column in range(0, width, 256):
        columns = slice(column, column + 256)
        moved = jnp.dot(select, placed[:, columns], preferred_element_type=F32).astype(BF16)
        mixed[:, columns] = jnp.where(owned, moved, mixed[:, columns])
    arrivals[2].wait()
    for column in range(0, width, 256):
        columns = slice(column, column + 256)
        out[:, columns] = jnp.dot(
            mixed[...], weight[2, :, columns], preferred_element_type=F32
        ).astype(BF16)


def last_call(shards, places, index, random_blocks, gain, gq, gold, queries, pieces, weights, parts, kv):
    rows, width = queries.shape
    keys = PICKS * BLOCK + NGLOB
    return call(
        functools.partial(last_kernel, shards, len(parts), places),
        [*index, random_blocks, gain, gq, gold, queries, *pieces, *weights, *parts, *kv],
        [SMEM, VMEM, SMEM] + [VMEM] * 4 + [HBM] * (5 + 2 * len(parts)),
        [((rows, width), BF16)],
        [VMEM],
        project_scratch(2, rows, width, 3)
        + [
            pltpu.VMEM((2, keys, 2 * width), BF16),
            pltpu.VMEM((rows, width), BF16),
            pltpu.VMEM((NGLOB, width), BF16),
            pltpu.VMEM((len(parts), 3, NGLOB, width), F32),
            pltpu.SemaphoreType.DMA((2, PICKS)),
            pltpu.SemaphoreType.DMA((NGLOB // TILE, len(parts))),
        ],
        "last",
    )[0]


def exchange(value, even, odd):
    count = lax.axis_size("seq")
    return lax.ppermute(value, "seq", [(i, i ^ (odd if i & 1 else even)) for i in range(count)])


def body(
    tokens,
    norm_gain,
    query_weight,
    key_weight,
    value_weight,
    out_weight,
    random_blocks,
    bucket_id,
    global_positions,
):
    shards = lax.axis_size("seq")
    width = tokens.shape[1]
    gain = norm_gain.reshape(1, width)
    pair = [key_weight, value_weight]
    index = [bucket_id, global_positions]
    steps = shards // 2
    if shards == 8:
        arrived = [tokens, exchange(tokens, 2, 4), exchange(tokens, 4, 2), None]
    else:
        arrived = [tokens] + [None] * (steps - 1)
        bit = 1
        while bit < steps:
            for step in range(bit):
                arrived[step | bit] = exchange(arrived[step], 2 * bit, 2 * bit)
            bit *= 2
    across = [exchange(tokens, 1, 1)]
    kv0, gsum, part, queries, gq = rows_call(
        shards, [(0, 0), (0, 1)], index, gain, [tokens, across[0]], [*pair, query_weight]
    )
    kv = [kv0]
    parts = [part]
    held, *arrived[1:3] = lax.optimization_barrier((gsum, *arrived[1:3]))
    if shards == 8:
        arrived[3] = exchange(arrived[1], 4, 2)
    pieces = []
    for step in range(1, steps - 1):
        pieces += [((step, 0), arrived[step]), ((step, 1), exchange(arrived[step], 1, 1))]
    for at in range(0, len(pieces), 4):
        some = pieces[at : at + 4]
        now, held, part = rows_call(
            shards, [p for p, _ in some], index, gain, [v for _, v in some], pair, gq, held
        )
        kv.append(now)
        parts.append(part)
    fresh, held = lax.optimization_barrier((arrived[-1], held))
    return last_call(
        shards,
        [(steps - 1, 0), (steps - 1, 1)],
        index,
        random_blocks,
        gain,
        gq,
        held,
        queries,
        [fresh, exchange(fresh, 1, 1)],
        [*pair, out_weight],
        parts,
        kv,
    )


def solution(mesh):
    placed = (P(("dp", "seq"), None), P(), P(), P(), P(), P(), P("dp", None), P(), P())
    return jax.shard_map(
        body, mesh=mesh, in_specs=placed, out_specs=P(("dp", "seq"), None), check_vma=False
    )
```

time: 271 us -> 81.5 us (0.30)
  local copies, waits for them, and re-layouts: 74.2 us -> 3.73 us
  waiting for transfers between devices: 76.3 us -> 7.66 us
  Pallas kernels: 0 us -> 61.9 us
  matrix products: 46.6 us -> 0 us
  other arithmetic: 31.5 us -> 0 us
  blocking collectives: 17.6 us -> 0 us
  between operations: 14.4 us -> 0.89 us
    psum x1 -> x0, waiting for transfers between devices: 71 us -> none  [body(): lax.psum(jnp.dot(selector, normed, preferred_element_type=jnp.float32).as...]
    pallas_call x0 -> x3, Pallas kernels: none -> 61.9 us  [call(): pl.pallas_call(kernel, out_shape=[jax.ShapeDtypeStruct(*out) for out in o...]
    dot_general x11 -> x0, matrix products: 36.2 us -> none  [the longest x1 10.9 us: body(): jnp.einsum('bhqk,bkhd->bqhd', probs, value_part, preferred_element_type=j...]
    slice x11 -> x0, local copies, waits for them, and re-layouts: 34.8 us -> none  [the longest x2 17.8 us: body(): key_part = key_set[:, :, :width].reshape(local_blocks, count, HEADS, HDIM)]
    all_gather x2 -> x0, blocking collectives: 17.6 us -> none  [combined_all(): pieces = jax.tree.map(lambda part: lax.all_gather(part, axis), value)]
    concatenate x4 -> x0, other arithmetic: 15.4 us -> none  [the longest x1 7.77 us: body(): key_set = jnp.concatenate([window, random_rows, global_broad], axis=1)]
    gather x2 -> x0, local copies, waits for them, and re-layouts: 13.4 us -> none  [the longest x1 7.37 us: body(): random_rows = incoming[my_source * capacity + my_rank]]
    sub x1 -> x0, matrix products: 10.5 us -> none  [body(): expo = jnp.exp(scores - top_score)]
  transfers between devices with their start and end apart: 5 -> 7, of which waited for: 3 -> 5; matrix products, arithmetic and copies ran while one was open for 38% -> 1% of each run, Pallas kernels for 0% -> 45%
where the time goes in v2:
time: 81.5 us; the launch traced here: 81.2 us
  Pallas kernels  61.9 us (76%)
  waiting for transfers between devices  7.66 us (9%)
  starting transfers between devices  6.98 us (9%)
  local copies, waits for them, and re-layouts  3.73 us (5%)
  between operations  0.89 us (1%)
    pallas_call x3, Pallas kernels, call(): pl.pallas_call(kernel, out_shape=[jax.ShapeDtypeStruct(*out) for out in o...  61.9 us
    ppermute x7, waiting for transfers between devices, exchange(): lax.ppermute(value, 'seq', [(i, i ^ (odd if i & 1 else even)) for i in ra...  7.66 us
    ppermute x7, starting transfers between devices, exchange(): lax.ppermute(value, 'seq', [(i, i ^ (odd if i & 1 else even)) for i in ra...  6.98 us
    unnamed x17, local copies, waits for them, and re-layouts  3.73 us
  transfers between devices with their start and end apart: 7, of which 5 were waited for; matrix products, arithmetic and copies ran while one was open for 1% of the time, Pallas kernels for 45%

profile of v2, /device:TPU:0, one launch (start us, length us, event | category | flops | bytes accessed | tf_op | source)
XLA Modules:
  0.0 81.2 jit_solution(1429998243976185560)
XLA Ops:
  0.0 0.5 collective-permute-start
  0.5 2.5 %collective-permute-start.1 = (bf16[512,1024]{1,0:T(8,128)(2,1)}, bf16[512,1024]{1,0:T(8,128)(2,1)S(1)}, u32[]{:S(2)}, u32[]{:S(2)}) collective-permute-start(bf16[512,1024]{1,0:T(8,128)(2,1)} %refs_3_.1), channel_id=1, source_target_pairs={{0,8},{4,20},{8,0},{12,28},{16,24},{20,4},{24,16},{28,12},{1,9},{5... | collective-permute-start | bytes 3145736 | tf_op jit(solution)/shard_map/ppermute | solution.py:459
  2.9 1.5 %collective-permute-start.2 = (bf16[512,1024]{1,0:T(8,128)(2,1)}, bf16[512,1024]{1,0:T(8,128)(2,1)S(1)}, u32[]{:S(2)}, u32[]{:S(2)}) collective-permute-start(bf16[512,1024]{1,0:T(8,128)(2,1)} %refs_3_.1), channel_id=1, source_target_pairs={{0,16},{4,12},{8,24},{12,4},{16,0},{20,28},{24,8},{28,20},{1,17},{... | collective-permute-start | bytes 3145736 | tf_op jit(solution)/shard_map/ppermute | solution.py:459
  5.1 0.0 collective-permute-done.refs_4_
  5.1 0.0 copy-start.1
  5.1 1.0 %copy-done.1 = bf16[512,1024]{1,0:T(8,128)(2,1)} copy-done((bf16[512,1024]{1,0:T(8,128)(2,1)}, bf16[512,1024]{1,0:T(8,128)(2,1)S(1)}, u32[]{:S(2)}) %copy-start.1) | copy-done | bytes 1048600
  6.1 16.8 %first.1 = (bf16[1024,2048]{1,0:T(8,128)(2,1)}, bf16[128,2048]{1,0:T(8,128)(2,1)}, f32[3,128,1024]{2,1,0:T(8,128)}, bf16[512,1024]{1,0:T(8,128)(2,1)}, bf16[128,1024]{1,0:T(8,128)(2,1)}) custom-call(s32[1]{0:T(128)S(6)} %copy.11.refs_0_, s32[8,128]{1,0:T(8,128)} %refs_1_.5, f32[1,1024]{1,0:T(1,128)} %bitcast.1, bf16[512,1024]{1,0:T(8,128)(2,1)} %refs_3_.1, ...), custom_call_target="tpu_custom_call" | custom-call | flops 1024 | bytes 1024 | tf_op jit(solution)/shard_map/first/pallas_call | solution.py:269
  22.9 3.1 %collective-permute-done.1.refs_3_ = bf16[512,1024]{1,0:T(8,128)(2,1)S(1)} collective-permute-done((bf16[512,1024]{1,0:T(8,128)(2,1)}, bf16[512,1024]{1,0:T(8,128)(2,1)S(1)}, u32[]{:S(2)}, u32[]{:S(2)}) %collective-permute-start.1) | collective-permute-done | bytes 1048608 | tf_op jit(solution)/shard_map/ppermute | solution.py:459
  26.1 0.0 copy-start.3
  26.1 0.9 %collective-permute-done.2.refs_5_ = bf16[512,1024]{1,0:T(8,128)(2,1)S(1)} collective-permute-done((bf16[512,1024]{1,0:T(8,128)(2,1)}, bf16[512,1024]{1,0:T(8,128)(2,1)S(1)}, u32[]{:S(2)}, u32[]{:S(2)}) %collective-permute-start.2) | collective-permute-done | bytes 1048608 | tf_op jit(solution)/shard_map/ppermute | solution.py:459
  27.0 0.0 copy-start.4
  27.0 0.1 collective-permute-start.4
  27.1 0.4 collective-permute-start.5
  27.5 1.8 %collective-permute-start.3 = (bf16[512,1024]{1,0:T(8,128)(2,1)S(1)}, bf16[512,1024]{1,0:T(8,128)(2,1)S(1)}, u32[]{:S(2)}, u32[]{:S(2)}) collective-permute-start(bf16[512,1024]{1,0:T(8,128)(2,1)S(1)} %collective-permute-done.1.refs_3_), channel_id=1, source_target_pairs={{0,16},{4,12},{8,24},{12,4},{16,0},{20,28},{24,8},{28,20},{1,17},{... | collective-permute-start | bytes 3145736 | tf_op jit(solution)/shard_map/ppermute | solution.py:459
  29.3 0.3 collective-permute-done.4.refs_4_
  29.7 0.0 copy-start.5
  29.7 1.5 %collective-permute-done.5.refs_6_ = bf16[512,1024]{1,0:T(8,128)(2,1)S(1)} collective-permute-done((bf16[512,1024]{1,0:T(8,128)(2,1)S(1)}, bf16[512,1024]{1,0:T(8,128)(2,1)S(1)}, u32[]{:S(2)}, u32[]{:S(2)}) %collective-permute-start.5) | collective-permute-done | bytes 1048608 | tf_op jit(solution)/shard_map/ppermute | solution.py:459
  31.2 0.0 copy-done.5
  31.2 0.0 copy-start.6
  31.2 1.0 %copy-done.6 = bf16[512,1024]{1,0:T(8,128)(2,1)} copy-done((bf16[512,1024]{1,0:T(8,128)(2,1)}, bf16[512,1024]{1,0:T(8,128)(2,1)S(1)}, u32[]{:S(2)}) %copy-start.6) | copy-done | bytes 1048600
  32.1 0.0 copy-done.3
  32.1 0.0 copy-done.4
  32.2 20.0 %middle.1 = (bf16[2048,2048]{1,0:T(8,128)(2,1)}, bf16[128,2048]{1,0:T(8,128)(2,1)}, f32[3,128,1024]{2,1,0:T(8,128)}) custom-call(s32[1]{0:T(128)S(6)} %copy.11.refs_0_, s32[8,128]{1,0:T(8,128)} %refs_1_.5, f32[1,1024]{1,0:T(1,128)} %bitcast.2, bf16[512,1024]{1,0:T(8,128)(2,1)} %copy-done.3, bf16[512,1024]{1,0:T(8,128)(2,1)} %copy-done.5, ...), custom_call_target="tpu_custom_call" | custom-call | flops 1024 | bytes 1024 | tf_op jit(solution)/shard_map/middle/pallas_call | solution.py:269
  52.2 0.0 collective-permute-done.3.refs_7_
  52.2 0.0 copy-start
  52.2 0.2 collective-permute-start.6
  52.4 0.0 copy-done.7
  52.4 0.8 copy.10.refs_2_
  53.2 1.7 %collective-permute-done.6.refs_8_ = bf16[512,1024]{1,0:T(8,128)(2,1)S(1)} collective-permute-done((bf16[512,1024]{1,0:T(8,128)(2,1)S(1)}, bf16[512,1024]{1,0:T(8,128)(2,1)S(1)}, u32[]{:S(2)}, u32[]{:S(2)}) %collective-permute-start.6) | collective-permute-done | bytes 1048608 | tf_op jit(solution)/shard_map/ppermute | solution.py:459
  54.9 0.0 copy-done
  54.9 1.0 %copy-done.2 = bf16[512,1024]{1,0:T(8,128)(2,1)} copy-done((bf16[512,1024]{1,0:T(8,128)(2,1)}, bf16[512,1024]{1,0:T(8,128)(2,1)S(1)}, u32[]{:S(2)}) %copy-start.2) | copy-done | bytes 1048600
  55.9 25.0 %last.1 = bf16[512,1024]{1,0:T(8,128)(2,1)} custom-call(s32[1]{0:T(128)S(6)} %copy.11.refs_0_, s32[8,128]{1,0:T(8,128)} %refs_1_.5, s32[64,3]{1,0:T(8,128)} %copy.10.refs_2_, f32[1,1024]{1,0:T(1,128)} %bitcast.3, bf16[128,1024]{1,0:T(8,128)(2,1)} %get-tuple-element.18.refs_9_.refs_4_, bf16[128,2048]{1,0:T(8,128)(2,1)} %get-tuple-element.24.refs_5_, ...), custom_call_target="tpu_custom_call" | custom-call | flops 1024 | bytes 1024 | tf_op jit(solution)/shard_map/last/pallas_call | solution.py:269
  (2 shorter events, 0.0 us)
Async XLA Ops:
  0.0 5.1 %collective-permute-start = (bf16[512,1024]{1,0:T(8,128)(2,1)}, bf16[512,1024]{1,0:T(8,128)(2,1)S(1)}, u32[]{:S(2)}, u32[]{:S(2)}) collective-permute-start(bf16[512,1024]{1,0:T(8,128)(2,1)} %refs_3_.1), channel_id=1, source_target_pairs={{0,4},{4,0},{8,12},{12,8},{16,20},{20,16},{24,28},{28,24},{1,5},{5... | collective-permute-start | bytes 3145736 | tf_op jit(solution)/shard_map/ppermute | solution.py:459
  0.5 25.6 %collective-permute-start.1 = (bf16[512,1024]{1,0:T(8,128)(2,1)}, bf16[512,1024]{1,0:T(8,128)(2,1)S(1)}, u32[]{:S(2)}, u32[]{:S(2)}) collective-permute-start(bf16[512,1024]{1,0:T(8,128)(2,1)} %refs_3_.1), channel_id=1, source_target_pairs={{0,8},{4,20},{8,0},{12,28},{16,24},{20,4},{24,16},{28,12},{1,9},{5... | collective-permute-start | bytes 3145736 | tf_op jit(solution)/shard_map/ppermute | solution.py:459
  2.9 24.1 %collective-permute-start.2 = (bf16[512,1024]{1,0:T(8,128)(2,1)}, bf16[512,1024]{1,0:T(8,128)(2,1)S(1)}, u32[]{:S(2)}, u32[]{:S(2)}) collective-permute-start(bf16[512,1024]{1,0:T(8,128)(2,1)} %refs_3_.1), channel_id=1, source_target_pairs={{0,16},{4,12},{8,24},{12,4},{16,0},{20,28},{24,8},{28,20},{1,17},{... | collective-permute-start | bytes 3145736 | tf_op jit(solution)/shard_map/ppermute | solution.py:459
  5.1 1.0 %copy-start.1 = (bf16[512,1024]{1,0:T(8,128)(2,1)}, bf16[512,1024]{1,0:T(8,128)(2,1)S(1)}, u32[]{:S(2)}) copy-start(bf16[512,1024]{1,0:T(8,128)(2,1)S(1)} %collective-permute-done.refs_4_) | copy-start | bytes 3145732
  26.1 6.1 %copy-start.3 = (bf16[512,1024]{1,0:T(8,128)(2,1)}, bf16[512,1024]{1,0:T(8,128)(2,1)S(1)}, u32[]{:S(2)}) copy-start(bf16[512,1024]{1,0:T(8,128)(2,1)S(1)} %collective-permute-done.1.refs_3_) | copy-start | bytes 3145732
  27.0 5.1 %copy-start.4 = (bf16[512,1024]{1,0:T(8,128)(2,1)}, bf16[512,1024]{1,0:T(8,128)(2,1)S(1)}, u32[]{:S(2)}) copy-start(bf16[512,1024]{1,0:T(8,128)(2,1)S(1)} %collective-permute-done.2.refs_5_) | copy-start | bytes 3145732
  27.0 2.7 %collective-permute-start.4 = (bf16[512,1024]{1,0:T(8,128)(2,1)S(1)}, bf16[512,1024]{1,0:T(8,128)(2,1)S(1)}, u32[]{:S(2)}, u32[]{:S(2)}) collective-permute-start(bf16[512,1024]{1,0:T(8,128)(2,1)S(1)} %collective-permute-done.1.refs_3_), channel_id=1, source_target_pairs={{0,4},{4,0},{8,12},{12,8},{16,20},{20,16},{24,28},{28,24},{1,5},{5... | collective-permute-start | bytes 3145736 | tf_op jit(solution)/shard_map/ppermute | solution.py:459
  27.1 4.0 %collective-permute-start.5 = (bf16[512,1024]{1,0:T(8,128)(2,1)S(1)}, bf16[512,1024]{1,0:T(8,128)(2,1)S(1)}, u32[]{:S(2)}, u32[]{:S(2)}) collective-permute-start(bf16[512,1024]{1,0:T(8,128)(2,1)S(1)} %collective-permute-done.2.refs_5_), channel_id=1, source_target_pairs={{0,4},{4,0},{8,12},{12,8},{16,20},{20,16},{24,28},{28,24},{1,5},{5... | collective-permute-start | bytes 3145736 | tf_op jit(solution)/shard_map/ppermute | solution.py:459
  27.5 24.7 %collective-permute-start.3 = (bf16[512,1024]{1,0:T(8,128)(2,1)S(1)}, bf16[512,1024]{1,0:T(8,128)(2,1)S(1)}, u32[]{:S(2)}, u32[]{:S(2)}) collective-permute-start(bf16[512,1024]{1,0:T(8,128)(2,1)S(1)} %collective-permute-done.1.refs_3_), channel_id=1, source_target_pairs={{0,16},{4,12},{8,24},{12,4},{16,0},{20,28},{24,8},{28,20},{1,17},{... | collective-permute-start | bytes 3145736 | tf_op jit(solution)/shard_map/ppermute | solution.py:459
  29.7 1.5 %copy-start.5 = (bf16[512,1024]{1,0:T(8,128)(2,1)}, bf16[512,1024]{1,0:T(8,128)(2,1)S(1)}, u32[]{:S(2)}) copy-start(bf16[512,1024]{1,0:T(8,128)(2,1)S(1)} %collective-permute-done.4.refs_4_) | copy-start | bytes 3145732
  31.2 1.0 %copy-start.6 = (bf16[512,1024]{1,0:T(8,128)(2,1)}, bf16[512,1024]{1,0:T(8,128)(2,1)S(1)}, u32[]{:S(2)}) copy-start(bf16[512,1024]{1,0:T(8,128)(2,1)S(1)} %collective-permute-done.5.refs_6_) | copy-start | bytes 3145732
  32.2 20.3 %copy-start.7 = (s32[64,3]{0,1:T(4,128)S(1)}, s32[64,3]{0,1:T(4,128)}, u32[]{:S(2)}) copy-start(s32[64,3]{0,1:T(4,128)} %param.15) | copy-start | bytes 2308
  52.2 2.7 %copy-start = (bf16[512,1024]{1,0:T(8,128)(2,1)}, bf16[512,1024]{1,0:T(8,128)(2,1)S(1)}, u32[]{:S(2)}) copy-start(bf16[512,1024]{1,0:T(8,128)(2,1)S(1)} %collective-permute-done.3.refs_7_) | copy-start | bytes 3145732
  52.2 2.7 %collective-permute-start.6 = (bf16[512,1024]{1,0:T(8,128)(2,1)S(1)}, bf16[512,1024]{1,0:T(8,128)(2,1)S(1)}, u32[]{:S(2)}, u32[]{:S(2)}) collective-permute-start(bf16[512,1024]{1,0:T(8,128)(2,1)S(1)} %collective-permute-done.3.refs_7_), channel_id=1, source_target_pairs={{0,4},{4,0},{8,12},{12,8},{16,20},{20,16},{24,28},{28,24},{1,5},{5... | collective-permute-start | bytes 3145736 | tf_op jit(solution)/shard_map/ppermute | solution.py:459
  54.9 1.0 %copy-start.2 = (bf16[512,1024]{1,0:T(8,128)(2,1)}, bf16[512,1024]{1,0:T(8,128)(2,1)S(1)}, u32[]{:S(2)}) copy-start(bf16[512,1024]{1,0:T(8,128)(2,1)S(1)} %collective-permute-done.6.refs_8_) | copy-start | bytes 3145732

commit v3 on v2

v3 whole, which is shorter than its diff:
```python
import functools
import math

import jax
import jax.numpy as jnp
from jax import lax
from jax.experimental import pallas as pl
from jax.experimental.pallas import tpu as pltpu
from jax.sharding import PartitionSpec as P

HEADS = 16
HDIM = 64
BLOCK = 64
RAND = 3
NGLOB = 128
GROUP = 4
GW = GROUP * HDIM
TILE = 32
CHUNK = 256
PICKS = 3 + RAND
EXP2 = HDIM ** (-0.5) * math.log2(math.e)
F32 = jnp.float32
BF16 = jnp.bfloat16
HBM = pl.BlockSpec(memory_space=pltpu.HBM)
VMEM = pl.BlockSpec(memory_space=pltpu.VMEM)
SMEM = pl.BlockSpec(memory_space=pltpu.SMEM)
LATE_COST = pl.CostEstimate(flops=10**11, bytes_accessed=1024, transcendentals=0)
COST = pl.CostEstimate(flops=1024, bytes_accessed=1024, transcendentals=0)


def params(mib):
    return pltpu.CompilerParams(vmem_limit_bytes=mib << 20)


LIMIT = 60


def hops_of(shards):
    if shards == 8:
        return [(0, 0), (2, 4), (4, 2), (6, 6)]
    return [(2 * step, 2 * step) for step in range(shards // 2)]


def layer_norm(tokens, gain):
    values = tokens.astype(F32)
    center = values - jnp.mean(values, axis=-1, keepdims=True)
    spread = jnp.mean(center * center, axis=-1, keepdims=True)
    return (center * lax.rsqrt(spread + 1e-05) * gain).astype(BF16)


def head_lane(rows):
    return lax.broadcasted_iota(jnp.int32, (rows, GW), 1) // HDIM


def spread_heads(rows):
    lane = head_lane(rows.shape[0])
    masks = [(lane == head).astype(BF16) for head in range(GROUP)]
    return jnp.concatenate([rows * mask for mask in masks], axis=0)


def pick_heads(stacked, rows):
    lane = head_lane(rows)
    picked = stacked[(GROUP - 1) * rows :]
    for head in range(GROUP - 1):
        picked = jnp.where(lane == head, stacked[head * rows : (head + 1) * rows], picked)
    return picked


def contract_last(left, right):
    return lax.dot_general(left, right, (((1,), (1,)), ((), ())), preferred_element_type=F32)


def square(axis):
    return lax.broadcasted_iota(jnp.int32, (NGLOB, NGLOB), axis)


class Globals:
    def __init__(self, bucket, table, rows, core=0):
        self.me = lax.axis_index("seq") ^ core
        self.rows = rows
        self.row = table[pl.ds(bucket[0], 1), :]
        self.local = self.row - self.me * rows
        self.first = jnp.sum((self.local < 0).astype(F32)).astype(jnp.int32)
        below = jnp.sum((self.local < rows).astype(F32)).astype(jnp.int32)
        self.count = below - self.first
        self.tiles = (self.count + TILE - 1) // TILE

    def column(self):
        spread = jnp.where(square(0) == square(1), self.row, 0).astype(F32)
        return jnp.sum(spread, axis=1, keepdims=True).astype(jnp.int32)

    def own_column(self):
        hit = jnp.where(square(1) == square(0) + self.first, self.local, 0).astype(F32)
        found = jnp.sum(hit, axis=1, keepdims=True).astype(jnp.int32)
        index = lax.broadcasted_iota(jnp.int32, (NGLOB, 1), 0)
        return jnp.where(index < self.count, found, -1)

    def own_row(self):
        local = self.column() - self.me * self.rows
        hit = jnp.where(square(0) == square(1) + self.first, local, 0).astype(F32)
        found = jnp.sum(hit, axis=0, keepdims=True).astype(jnp.int32)
        index = lax.broadcasted_iota(jnp.int32, (1, NGLOB), 1)
        return jnp.where(index < self.count, found, -1)


def owner(me, step, core, shards):
    even, odd = hops_of(shards)[step]
    there = me ^ core
    return there ^ jnp.where(there & 1 == 0, even, odd)


def place_of(device, me, shards):
    slot = device ^ me
    core = slot & 1
    hop = slot - core
    if shards != 8:
        return hop // 2, core
    parity = (me ^ core) & 1
    near = jnp.where((hop == 2) == (parity == 0), 1, 2)
    return jnp.where(hop == 0, 0, jnp.where(hop == 6, 3, near)), core


def start_loads(sources, targets, sems):
    loads = []
    for index, (source, target) in enumerate(zip(sources, targets)):
        load = pltpu.make_async_copy(source, target, sems.at[index])
        load.start()
        loads.append(load)
    return loads


def select_rows(info, bases, rows):
    lane = lax.broadcasted_iota(jnp.int32, (1, len(bases) * rows), 1)
    column = info.column()
    where = jnp.full((NGLOB, 1), -1, jnp.int32)
    for piece, base in enumerate(bases):
        inside = column - base * rows
        hit = jnp.where(inside < 0, rows, inside) < rows
        where = jnp.where(hit, inside + piece * rows, where)
    return (where == lane).astype(BF16)


def norm_chunk(tokens, gain, normed, at):
    rows = tokens.shape[1]
    piece, start = at // rows, at % rows
    for row in range(0, CHUNK, 64):
        normed[at + row : at + row + 64, :] = layer_norm(
            tokens[piece, start + row : start + row + 64, :], gain[...]
        )


def multiply(normed, at, height, weights, results):
    left = normed[at : at + height, :]
    width = normed.shape[1]
    for index, weight in enumerate(weights):
        for start in range(0, width, 256):
            results[at : at + height, index * width + start : index * width + start + 256] = (
                jnp.dot(
                    left, weight[:, start : start + 256], preferred_element_type=F32
                ).astype(BF16)
            )


def global_partial(tiles, queries, kv, total, scores, states):
    width = queries[0].shape[1]
    stacked = GROUP * TILE
    count = len(queries)

    def one_tile(tile, carry):
        at = pl.ds(pl.multiple_of(tile * TILE, TILE), TILE)
        for group in range(width // GW):
            columns = slice(group * GW, (group + 1) * GW)
            values = slice(width + group * GW, width + (group + 1) * GW)
            left = [spread_heads(ref[at, columns]) for ref in queries]
            left = left[0] if count == 1 else jnp.concatenate(left, axis=0)
            scores[...] = contract_last(left, kv[:total, columns])
            top = jnp.max(scores[...], axis=1, keepdims=True)
            probs = jnp.exp2((scores[...] - top) * EXP2)
            part = jnp.sum(probs, axis=1, keepdims=True)
            acc = jnp.dot(probs.astype(BF16), kv[:total, values], preferred_element_type=F32)
            shape = (count * stacked, GW)
            for index, value in enumerate(
                (jnp.broadcast_to(top, shape), jnp.broadcast_to(part, shape), acc)
            ):
                for which, state in enumerate(states):
                    state[index, at, columns] = pick_heads(
                        value[which * stacked : (which + 1) * stacked], TILE
                    )
        return carry

    lax.fori_loop(0, tiles, one_tile, 0)


def move_state(tiles, pairs, sems, act):
    for tile in range(NGLOB // TILE):

        @pl.when(tile < tiles)
        def _():
            rows = slice(tile * TILE, (tile + 1) * TILE)
            for index, (source, target) in enumerate(pairs):
                copy = pltpu.make_async_copy(
                    source.at[:, rows, :], target.at[:, rows, :], sems.at[tile, index]
                )
                copy.start() if act == "start" else copy.wait()


def merge_states(tiles, states, target):
    def one_tile(tile, carry):
        at = pl.ds(pl.multiple_of(tile * TILE, TILE), TILE)
        top = functools.reduce(jnp.maximum, [ref[0, at, :] for ref in states])
        total = jnp.zeros_like(top)
        acc = jnp.zeros_like(top)
        for ref in states:
            factor = jnp.exp2((ref[0, at, :] - top) * EXP2)
            total += ref[1, at, :] * factor
            acc += ref[2, at, :] * factor
        target[at, :] = (acc / total).astype(BF16)
        return carry

    lax.fori_loop(0, tiles, one_tile, 0)


def rows_kernel(shards, places, kind, *refs):
    count = len(places)
    first = kind == "first"
    sets = 2 if kind == "middle" else 1
    refs = list(refs)

    def take(number):
        taken = refs[:number]
        del refs[:number]
        return taken

    bucket, table, gain = take(3)
    sources = take(count)
    weights = take(2 + first)
    gq_sets = take(0 if first else sets)
    out, gsum = take(2)
    kept = take(sets)
    if first:
        (queries,) = take(1)
        gq_sets = take(1)
    tokens, weight, normed, results, token_sems, weight_sems, out_sems, sems, scores = take(9)
    states = take(sets)
    rows, width = sources[0].shape
    total = count * rows
    loads = start_loads(sources, [tokens.at[i] for i in range(count)], token_sems)
    arrivals = start_loads(weights, [weight.at[i] for i in range(len(weights))], weight_sems)
    info = Globals(bucket, table, rows)
    bases = [owner(info.me, step, core, shards) for step, core in places]
    select = select_rows(info, bases, rows)
    loads[0].wait()
    norm_chunk(tokens, gain, normed, 0)
    for load in loads[1:] + arrivals:
        load.wait()
    pair = [weight.at[0], weight.at[1]]
    stores = []
    for at in range(0, total, CHUNK):
        if at + CHUNK < total:
            norm_chunk(tokens, gain, normed, at + CHUNK)
        multiply(normed, at, CHUNK, pair, results)
        store = pltpu.make_async_copy(
            results.at[at : at + CHUNK, :], out.at[at : at + CHUNK, :], out_sems.at[at // CHUNK]
        )
        store.start()
        stores.append(store)
    for start in range(0, width, 256):
        columns = slice(start, start + 256)
        normed[total:, columns] = jnp.dot(
            select, normed[:total, columns], preferred_element_type=F32
        ).astype(BF16)
    multiply(normed, total, NGLOB, pair, results)
    gsum[...] = results[total:, :]
    if first:
        lane = lax.broadcasted_iota(jnp.int32, (1, rows), 1)
        own = (info.own_column() == lane).astype(BF16)
        for start in range(0, width, 256):
            columns = slice(start, start + 256)
            query = jnp.dot(
                normed[:rows, :], weight[2, :, columns], preferred_element_type=F32
            ).astype(BF16)
            queries[:, columns] = query
            gq_sets[0][:, columns] = jnp.dot(
                own, query, preferred_element_type=F32
            ).astype(BF16)
    tiles = info.tiles
    if kind == "middle":
        tiles = jnp.maximum(tiles, Globals(bucket, table, rows, 1).tiles)
    global_partial(tiles, gq_sets, results, total, scores, states)
    pairs = list(zip(states, kept))
    move_state(tiles, pairs, sems, "start")
    move_state(tiles, pairs, sems, "wait")
    for store in stores:
        store.wait()


def call(kernel, inputs, specs, outs, out_specs, scratch, name, cost=COST):
    return pl.pallas_call(
        kernel,
        out_shape=[jax.ShapeDtypeStruct(*out) for out in outs],
        in_specs=specs,
        out_specs=out_specs,
        scratch_shapes=scratch,
        compiler_params=params(LIMIT),
        cost_estimate=cost,
        name=name,
    )(*inputs)


def rows_call(shards, places, kind, index, gain, pieces, weights, *more):
    rows, width = pieces[0].shape
    count = len(pieces)
    first = kind == "first"
    sets = 2 if kind == "middle" else 1
    total = count * rows
    outs = [((total, 2 * width), BF16), ((NGLOB, 2 * width), BF16)]
    outs += [((3, NGLOB, width), F32)] * sets
    specs = [HBM, VMEM] + [HBM] * sets
    if first:
        outs += [((rows, width), BF16), ((NGLOB, width), BF16)]
        specs += [VMEM, VMEM]
    scratch = [
        pltpu.VMEM((count, rows, width), BF16),
        pltpu.VMEM((len(weights), width, width), BF16),
        pltpu.VMEM((total + NGLOB, width), BF16),
        pltpu.VMEM((total + NGLOB, 2 * width), BF16),
        pltpu.SemaphoreType.DMA((count,)),
        pltpu.SemaphoreType.DMA((len(weights),)),
        pltpu.SemaphoreType.DMA((total // CHUNK,)),
        pltpu.SemaphoreType.DMA((NGLOB // TILE, sets)),
        pltpu.VMEM((sets * GROUP * TILE, total), F32),
    ] + [pltpu.VMEM((3, NGLOB, width), F32)] * sets
    return call(
        functools.partial(rows_kernel, shards, places, kind),
        [*index, gain, *pieces, *weights, *more],
        [SMEM, VMEM, VMEM] + [HBM] * (count + len(weights)) + [VMEM] * len(more),
        outs,
        specs,
        scratch,
        kind,
        LATE_COST if kind == "late" else COST,
    )


def pick_table(random_blocks, rows, shards):
    me = lax.axis_index("seq").astype(jnp.int32)
    blocks = rows // BLOCK
    steps = shards // 2
    total = shards * blocks
    here = me * blocks + jnp.arange(blocks, dtype=jnp.int32)[:, None]
    window = lax.rem(here + total + jnp.arange(-1, 2, dtype=jnp.int32)[None, :], total)
    listed = lax.dynamic_slice_in_dim(random_blocks.astype(jnp.int32), me * blocks, blocks, 0)
    chosen = jnp.concatenate([window, listed], axis=1).reshape(-1)
    device = chosen // blocks
    step, core = place_of(device, me, shards)
    edge = (step == 0) | (step == steps - 1)
    piece = jnp.where(edge, core, step - 1)
    source = jnp.where(step == 0, 0, jnp.where(edge, 3, 1 + core))
    return source, piece * rows + (chosen - device * blocks) * BLOCK


def attend_kernel(shards, *refs):
    bucket, table, source_ref, start_ref, query_source, *g_sources, out_weight = refs[:10]
    part_refs = refs[10:14]
    kv_refs = refs[14:18]
    (out, queries, weight, tails, keys, mixed, placed, olds, result) = refs[18:27]
    sems, state_sems, load_sems, out_sems = refs[27:]
    rows, width = queries.shape
    blocks = rows // BLOCK
    span = PICKS * BLOCK
    info = Globals(bucket, table, rows)

    def copies(block, slot, act):
        for pick in range(PICKS):
            target = keys.at[slot, pl.ds(pick * BLOCK, BLOCK), :]
            sem = sems.at[slot, pick]
            if act == "wait":
                pltpu.make_async_copy(kv_refs[0].at[pl.ds(0, BLOCK), :], target, sem).wait()
                continue
            entry = block * PICKS + pick
            source = source_ref[entry]
            start = pl.multiple_of(start_ref[entry], BLOCK)
            for index, held in enumerate(kv_refs):

                @pl.when(source == index)
                def _():
                    pltpu.make_async_copy(held.at[pl.ds(start, BLOCK), :], target, sem).start()

    copies(0, 0, "start")
    loads = start_loads(
        [query_source, *g_sources, out_weight],
        [queries, *[tails.at[i] for i in range(4)], weight],
        load_sems,
    )
    mine_refs = [olds.at[i] for i in range(4)]
    pairs = list(zip(part_refs, mine_refs))
    move_state(info.tiles, pairs, state_sems, "start")
    placed[...] = jnp.zeros_like(placed)
    for load in loads[:5]:
        load.wait()
    gathered = (tails[0] + tails[1]) + (tails[2] + tails[3])
    keys[0, span:, :] = gathered
    keys[1, span:, :] = gathered

    def one_block(block, carry):
        slot = lax.rem(block, 2)

        @pl.when(block + 1 < blocks)
        def _():
            copies(block + 1, 1 - slot, "start")

        copies(block, slot, "wait")
        at = pl.ds(pl.multiple_of(block * BLOCK, BLOCK), BLOCK)
        groups = range(width // GW)
        score = [
            contract_last(
                spread_heads(queries[at, g * GW : (g + 1) * GW]),
                keys[slot, :, g * GW : (g + 1) * GW],
            )
            for g in groups
        ]
        probs = []
        totals = []
        for g in groups:
            top = jnp.max(score[g], axis=1, keepdims=True)
            prob = jnp.exp2((score[g] - top) * EXP2)
            totals.append(jnp.sum(prob, axis=1, keepdims=True))
            probs.append(prob.astype(BF16))
        for g in groups:
            weighted = jnp.dot(
                probs[g],
                keys[slot, :, width + g * GW : width + (g + 1) * GW],
                preferred_element_type=F32,
            )
            mixed[at, g * GW : (g + 1) * GW] = pick_heads(
                weighted * (1.0 / totals[g]), BLOCK
            ).astype(BF16)
        return carry

    lax.fori_loop(0, blocks, one_block, 0)
    move_state(info.tiles, pairs, state_sems, "wait")
    merge_states(info.tiles, mine_refs, placed)
    row = lax.broadcasted_iota(jnp.int32, (rows, NGLOB), 0)
    select = row == info.own_row()
    owned = jnp.max(select.astype(F32), axis=1, keepdims=True) > 0.5
    select = select.astype(BF16)
    for column in range(0, width, 256):
        columns = slice(column, column + 256)
        moved = jnp.dot(select, placed[:, columns], preferred_element_type=F32).astype(BF16)
        mixed[:, columns] = jnp.where(owned, moved, mixed[:, columns])
    loads[5].wait()
    for column in range(0, width, 256):
        columns = slice(column, column + 256)
        result[:, columns] = jnp.dot(
            mixed[...], weight[:, columns], preferred_element_type=F32
        ).astype(BF16)
        pltpu.make_async_copy(
            result.at[:, columns], out.at[:, columns], out_sems.at[column // 256]
        ).start()
    for column in range(0, width, 256):
        columns = slice(column, column + 256)
        pltpu.make_async_copy(
            result.at[:, columns], out.at[:, columns], out_sems.at[column // 256]
        ).wait()


def attend_call(shards, index, picks, queries, gsums, out_weight, parts, kv):
    rows, width = queries.shape
    keys = PICKS * BLOCK + NGLOB
    return call(
        functools.partial(attend_kernel, shards),
        [*index, *picks, queries, *gsums, out_weight, *parts, *kv],
        [SMEM, VMEM, SMEM, SMEM] + [HBM] * 14,
        [((rows, width), BF16)],
        [HBM],
        [
            pltpu.VMEM((rows, width), BF16),
            pltpu.VMEM((width, width), BF16),
            pltpu.VMEM((4, NGLOB, 2 * width), BF16),
            pltpu.VMEM((2, keys, 2 * width), BF16),
            pltpu.VMEM((rows, width), BF16),
            pltpu.VMEM((NGLOB, width), BF16),
            pltpu.VMEM((4, 3, NGLOB, width), F32),
            pltpu.VMEM((rows, width), BF16),
            pltpu.SemaphoreType.DMA((2, PICKS)),
            pltpu.SemaphoreType.DMA((NGLOB // TILE, 4)),
            pltpu.SemaphoreType.DMA((6,)),
            pltpu.SemaphoreType.DMA((width // 256,)),
        ],
        "attend",
    )[0]


def exchange(value, even, odd):
    count = lax.axis_size("seq")
    return lax.ppermute(value, "seq", [(i, i ^ (odd if i & 1 else even)) for i in range(count)])


def body(
    tokens,
    norm_gain,
    query_weight,
    key_weight,
    value_weight,
    out_weight,
    random_blocks,
    bucket_id,
    global_positions,
):
    shards = lax.axis_size("seq")
    width = tokens.shape[1]
    gain = norm_gain.reshape(1, width)
    pair = [key_weight, value_weight]
    index = [bucket_id, global_positions]
    steps = shards // 2
    if shards == 8:
        arrived = [tokens, exchange(tokens, 2, 4), exchange(tokens, 4, 2), None]
    else:
        arrived = [tokens] + [None] * (steps - 1)
        bit = 1
        while bit < steps:
            for step in range(bit):
                arrived[step | bit] = exchange(arrived[step], 2 * bit, 2 * bit)
            bit *= 2
    across = exchange(tokens, 1, 1)
    kv_own, g_first, s_first, queries, gq = rows_call(
        shards, [(0, 0), (0, 1)], "first", index, gain, [tokens, across], [*pair, query_weight]
    )
    gother = exchange(gq, 1, 1)
    picks = pick_table(random_blocks, tokens.shape[0], shards)
    kv_own, picks, *arrived[1:-1] = lax.optimization_barrier((kv_own, picks, *arrived[1:-1]))
    if shards == 8:
        arrived[3] = exchange(arrived[1], 4, 2)
    kv_mine, g_mine, s_mine, s_other = rows_call(
        shards,
        [(s, 0) for s in range(1, steps - 1)],
        "middle",
        index,
        gain,
        arrived[1:-1],
        pair,
        gq,
        gother,
    )
    kv_other, g_other = exchange(kv_mine, 1, 1), exchange(g_mine, 1, 1)
    s_mine, fresh = lax.optimization_barrier((s_mine, arrived[-1]))
    s_other = exchange(s_other, 1, 1)
    kv_late, g_late, s_late = rows_call(
        shards,
        [(steps - 1, 0), (steps - 1, 1)],
        "late",
        index,
        gain,
        [fresh, exchange(fresh, 1, 1)],
        pair,
        gq,
    )
    return attend_call(
        shards,
        index,
        picks,
        queries,
        [g_first, g_mine, g_other, g_late],
        out_weight,
        [s_first, s_mine, s_other, s_late],
        [kv_own, kv_mine, kv_other, kv_late],
    )


def solution(mesh):
    placed = (P(("dp", "seq"), None), P(), P(), P(), P(), P(), P("dp", None), P(), P())
    return jax.shard_map(
        body, mesh=mesh, in_specs=placed, out_specs=P(("dp", "seq"), None), check_vma=False
    )
```

time: 81.5 us -> 78.2 us (0.960)
  Pallas kernels: 61.9 us -> 58.5 us
  other arithmetic: 0 us -> 1.86 us
  waiting for transfers between devices: 7.66 us -> 5.91 us
    pallas_call x3 -> x4, Pallas kernels: 61.9 us -> 58.5 us  [call(): pl.pallas_call(kernel, out_shape=[jax.ShapeDtypeStruct(*out) for out in o...]
    ppermute x7 -> x9, waiting for transfers between devices: 7.66 us -> 5.91 us  [exchange(): lax.ppermute(value, 'seq', [(i, i ^ (odd if i & 1 else even)) for i in ra...]
    unnamed x17 -> x14, local copies, waits for them, and re-layouts: 3.73 us -> 3.02 us
    ppermute x7 -> x9, starting transfers between devices: 6.98 us -> 7.32 us  [exchange(): lax.ppermute(value, 'seq', [(i, i ^ (odd if i & 1 else even)) for i in ra...]
  transfers between devices with their start and end apart: 7 -> 9, of which waited for: 5 -> 4; matrix products, arithmetic and copies ran while one was open for 1% -> 3% of each run, Pallas kernels for 45% -> 55%
where the time goes in v3:
time: 78.2 us; the launch traced here: 77.7 us
  Pallas kernels  58.5 us (75%)
  starting transfers between devices  7.32 us (9%)
  waiting for transfers between devices  5.91 us (8%)
  local copies, waits for them, and re-layouts  3.18 us (4%)
  other arithmetic  1.86 us (2%)
  between operations  0.94 us (1%)
    pallas_call x4, Pallas kernels, call(): pl.pallas_call(kernel, out_shape=[jax.ShapeDtypeStruct(*out) for out in o...  58.5 us
    ppermute x9, starting transfers between devices, exchange(): lax.ppermute(value, 'seq', [(i, i ^ (odd if i & 1 else even)) for i in ra...  7.32 us
    ppermute x9, waiting for transfers between devices, exchange(): lax.ppermute(value, 'seq', [(i, i ^ (odd if i & 1 else even)) for i in ra...  5.91 us
    unnamed x14, local copies, waits for them, and re-layouts  3.02 us
  transfers between devices with their start and end apart: 9, of which 4 were waited for; matrix products, arithmetic and copies ran while one was open for 3% of the time, Pallas kernels for 55%

profile of v3, /device:TPU:0, one launch (start us, length us, event | category | flops | bytes accessed | tf_op | source)
XLA Modules:
  0.0 77.7 jit_solution(911963919696117553)
XLA Ops:
  0.0 0.5 collective-permute-start
  0.5 2.5 %collective-permute-start.2 = (bf16[512,1024]{1,0:T(8,128)(2,1)}, bf16[512,1024]{1,0:T(8,128)(2,1)S(1)}, u32[]{:S(2)}, u32[]{:S(2)}) collective-permute-start(bf16[512,1024]{1,0:T(8,128)(2,1)} %refs_3_.1), channel_id=1, source_target_pairs={{0,16},{4,12},{8,24},{12,4},{16,0},{20,28},{24,8},{28,20},{1,17},{... | collective-permute-start | bytes 3145736 | tf_op jit(solution)/shard_map/ppermute | solution.py:496
  3.0 1.5 %collective-permute-start.1 = (bf16[512,1024]{1,0:T(8,128)(2,1)}, bf16[512,1024]{1,0:T(8,128)(2,1)S(1)}, u32[]{:S(2)}, u32[]{:S(2)}) collective-permute-start(bf16[512,1024]{1,0:T(8,128)(2,1)} %refs_3_.1), channel_id=1, source_target_pairs={{0,8},{4,20},{8,0},{12,28},{16,24},{20,4},{24,16},{28,12},{1,9},{5... | collective-permute-start | bytes 3145736 | tf_op jit(solution)/shard_map/ppermute | solution.py:496
  5.1 0.8 negate_select_fusion
  5.9 0.1 copy.10
  6.0 0.1 reshape.18
  6.1 0.6 multiply_add_fusion
  6.6 0.5 compare_select_fusion.6.refs_2_
  7.2 0.0 collective-permute-done.refs_4_
  7.2 1.0 %copy-done.1 = bf16[512,1024]{1,0:T(8,128)(2,1)} copy-done((bf16[512,1024]{1,0:T(8,128)(2,1)}, bf16[512,1024]{1,0:T(8,128)(2,1)S(1)}, u32[]{:S(2)}) %copy-start.1) | copy-done | bytes 1048600
  8.1 16.6 %first.1 = (bf16[1024,2048]{1,0:T(8,128)(2,1)}, bf16[128,2048]{1,0:T(8,128)(2,1)}, f32[3,128,1024]{2,1,0:T(8,128)}, bf16[512,1024]{1,0:T(8,128)(2,1)}, bf16[128,1024]{1,0:T(8,128)(2,1)}) custom-call(s32[1]{0:T(128)S(6)} %copy.11.refs_0_, s32[8,128]{1,0:T(8,128)} %refs_1_.7, f32[1,1024]{1,0:T(1,128)} %bitcast.1, bf16[512,1024]{1,0:T(8,128)(2,1)} %refs_3_.1, ...), custom_call_target="tpu_custom_call" | custom-call | flops 1024 | bytes 1024 | tf_op jit(solution)/shard_map/first/pallas_call | solution.py:298
  24.7 1.4 %collective-permute-done.2.refs_4_ = bf16[512,1024]{1,0:T(8,128)(2,1)S(1)} collective-permute-done((bf16[512,1024]{1,0:T(8,128)(2,1)}, bf16[512,1024]{1,0:T(8,128)(2,1)S(1)}, u32[]{:S(2)}, u32[]{:S(2)}) %collective-permute-start.2) | collective-permute-done | bytes 1048608 | tf_op jit(solution)/shard_map/ppermute | solution.py:496
  26.1 0.9 %collective-permute-done.1.refs_3_ = bf16[512,1024]{1,0:T(8,128)(2,1)S(1)} collective-permute-done((bf16[512,1024]{1,0:T(8,128)(2,1)}, bf16[512,1024]{1,0:T(8,128)(2,1)S(1)}, u32[]{:S(2)}, u32[]{:S(2)}) %collective-permute-start.1) | collective-permute-done | bytes 1048608 | tf_op jit(solution)/shard_map/ppermute | solution.py:496
  27.0 1.8 %collective-permute-start.5 = (bf16[512,1024]{1,0:T(8,128)(2,1)S(1)}, bf16[512,1024]{1,0:T(8,128)(2,1)S(1)}, u32[]{:S(2)}, u32[]{:S(2)}) collective-permute-start(bf16[512,1024]{1,0:T(8,128)(2,1)S(1)} %collective-permute-done.1.refs_3_), channel_id=1, source_target_pairs={{0,16},{4,12},{8,24},{12,4},{16,0},{20,28},{24,8},{28,20},{1,17},{... | collective-permute-start | bytes 3145736 | tf_op jit(solution)/shard_map/ppermute | solution.py:496
  28.8 0.0 collective-permute-start.3
  28.8 1.7 %collective-permute-done.3.refs_8_ = bf16[128,1024]{1,0:T(8,128)(2,1)S(1)} collective-permute-done((bf16[128,1024]{1,0:T(8,128)(2,1)}, bf16[128,1024]{1,0:T(8,128)(2,1)S(1)}, u32[]{:S(2)}, u32[]{:S(2)}) %collective-permute-start.3) | collective-permute-done | bytes 262176 | tf_op jit(solution)/shard_map/ppermute | solution.py:496
  30.5 0.7 copy-done.5
  31.2 13.3 %middle.1 = (bf16[1024,2048]{1,0:T(8,128)(2,1)}, bf16[128,2048]{1,0:T(8,128)(2,1)}, f32[3,128,1024]{2,1,0:T(8,128)}, f32[3,128,1024]{2,1,0:T(8,128)}) custom-call(s32[1]{0:T(128)S(6)} %copy.11.refs_0_, s32[8,128]{1,0:T(8,128)} %refs_1_.7, f32[1,1024]{1,0:T(1,128)} %bitcast.2, bf16[512,1024]{1,0:T(8,128)(2,1)} %copy-done.3, bf16[512,1024]{1,0:T(8,128)(2,1)} %copy-done.2, ...), custom_call_target="tpu_custom_call" | custom-call | flops 1024 | bytes 1024 | tf_op jit(solution)/shard_map/middle/pallas_call | solution.py:298
  44.5 0.0 collective-permute-done.5.refs_3_
  44.6 0.0 copy-start.6
  44.6 0.2 collective-permute-start.6
  44.8 0.4 collective-permute-start.4
  45.1 0.1 collective-permute-start.7
  45.3 0.4 collective-permute-start.8
  45.7 1.9 %collective-permute-done.6.refs_4_ = bf16[512,1024]{1,0:T(8,128)(2,1)} collective-permute-done((bf16[512,1024]{1,0:T(8,128)(2,1)S(1)}, bf16[512,1024]{1,0:T(8,128)(2,1)}, u32[]{:S(2)}, u32[]{:S(2)}) %collective-permute-start.6) | collective-permute-done | bytes 1048608 | tf_op jit(solution)/shard_map/ppermute | solution.py:496
  47.5 12.8 %late.1 = (bf16[1024,2048]{1,0:T(8,128)(2,1)}, bf16[128,2048]{1,0:T(8,128)(2,1)}, f32[3,128,1024]{2,1,0:T(8,128)}) custom-call(s32[1]{0:T(128)S(6)} %copy.11.refs_0_, s32[8,128]{1,0:T(8,128)} %refs_1_.7, f32[1,1024]{1,0:T(1,128)} %bitcast.3, bf16[512,1024]{1,0:T(8,128)(2,1)} %copy-done.6, bf16[512,1024]{1,0:T(8,128)(2,1)} %collective-permute-done.6.refs_4_, ...), custom_call_target="tpu_custom_call" | custom-call | flops 99999997952 | bytes 1024 | tf_op jit(solution)/shard_map/late/pallas_call | solution.py:298
  60.4 0.0 collective-permute-done.4.refs_7_
  60.4 0.0 collective-permute-done.7.refs_12_
  60.4 0.0 collective-permute-done.8.refs_16_
  60.4 0.8 copy-done.4
  61.2 0.5 copy-done
  61.7 15.8 %attend.1 = bf16[512,1024]{1,0:T(8,128)(2,1)} custom-call(s32[1]{0:T(128)S(6)} %copy.11.refs_0_, s32[8,128]{1,0:T(8,128)} %refs_1_.7, s32[48]{0:T(128)} %compare_select_fusion.6.refs_2_, s32[48]{0:T(128)} %get-tuple-element.26.refs_3_, bf16[512,1024]{1,0:T(8,128)(2,1)} %get-tuple-element.27.refs_4_, bf16[128,2048]{1,0:T(8,128)(2,1)} %get-tuple-element.28.refs_5_, ...), custom_call_target="tpu_custom_call" | custom-call | flops 1024 | bytes 1024 | tf_op jit(solution)/shard_map/attend/pallas_call | solution.py:298
  (12 shorter events, 0.0 us)
Async XLA Ops:
  0.0 7.2 %collective-permute-start = (bf16[512,1024]{1,0:T(8,128)(2,1)}, bf16[512,1024]{1,0:T(8,128)(2,1)S(1)}, u32[]{:S(2)}, u32[]{:S(2)}) collective-permute-start(bf16[512,1024]{1,0:T(8,128)(2,1)} %refs_3_.1), channel_id=1, source_target_pairs={{0,4},{4,0},{8,12},{12,8},{16,20},{20,16},{24,28},{28,24},{1,5},{5... | collective-permute-start | bytes 3145736 | tf_op jit(solution)/shard_map/ppermute | solution.py:496
  0.5 25.7 %collective-permute-start.2 = (bf16[512,1024]{1,0:T(8,128)(2,1)}, bf16[512,1024]{1,0:T(8,128)(2,1)S(1)}, u32[]{:S(2)}, u32[]{:S(2)}) collective-permute-start(bf16[512,1024]{1,0:T(8,128)(2,1)} %refs_3_.1), channel_id=1, source_target_pairs={{0,16},{4,12},{8,24},{12,4},{16,0},{20,28},{24,8},{28,20},{1,17},{... | collective-permute-start | bytes 3145736 | tf_op jit(solution)/shard_map/ppermute | solution.py:496
  3.0 24.0 %collective-permute-start.1 = (bf16[512,1024]{1,0:T(8,128)(2,1)}, bf16[512,1024]{1,0:T(8,128)(2,1)S(1)}, u32[]{:S(2)}, u32[]{:S(2)}) collective-permute-start(bf16[512,1024]{1,0:T(8,128)(2,1)} %refs_3_.1), channel_id=1, source_target_pairs={{0,8},{4,20},{8,0},{12,28},{16,24},{20,4},{24,16},{28,12},{1,9},{5... | collective-permute-start | bytes 3145736 | tf_op jit(solution)/shard_map/ppermute | solution.py:496
  7.2 1.0 %copy-start.1 = (bf16[512,1024]{1,0:T(8,128)(2,1)}, bf16[512,1024]{1,0:T(8,128)(2,1)S(1)}, u32[]{:S(2)}) copy-start(bf16[512,1024]{1,0:T(8,128)(2,1)S(1)} %collective-permute-done.refs_4_) | copy-start | bytes 3145732
  26.1 4.4 %copy-start.2 = (bf16[512,1024]{1,0:T(8,128)(2,1)}, bf16[512,1024]{1,0:T(8,128)(2,1)S(1)}, u32[]{:S(2)}) copy-start(bf16[512,1024]{1,0:T(8,128)(2,1)S(1)} %collective-permute-done.2.refs_4_) | copy-start | bytes 3145732
  27.0 3.5 %copy-start.3 = (bf16[512,1024]{1,0:T(8,128)(2,1)}, bf16[512,1024]{1,0:T(8,128)(2,1)S(1)}, u32[]{:S(2)}) copy-start(bf16[512,1024]{1,0:T(8,128)(2,1)S(1)} %collective-permute-done.1.refs_3_) | copy-start | bytes 3145732
  27.0 17.6 %collective-permute-start.5 = (bf16[512,1024]{1,0:T(8,128)(2,1)S(1)}, bf16[512,1024]{1,0:T(8,128)(2,1)S(1)}, u32[]{:S(2)}, u32[]{:S(2)}) collective-permute-start(bf16[512,1024]{1,0:T(8,128)(2,1)S(1)} %collective-permute-done.1.refs_3_), channel_id=1, source_target_pairs={{0,16},{4,12},{8,24},{12,4},{16,0},{20,28},{24,8},{28,20},{1,17},{... | collective-permute-start | bytes 3145736 | tf_op jit(solution)/shard_map/ppermute | solution.py:496
  28.8 1.7 %collective-permute-start.3 = (bf16[128,1024]{1,0:T(8,128)(2,1)}, bf16[128,1024]{1,0:T(8,128)(2,1)S(1)}, u32[]{:S(2)}, u32[]{:S(2)}) collective-permute-start(bf16[128,1024]{1,0:T(8,128)(2,1)} %get-tuple-element.31.refs_7_), channel_id=1, source_target_pairs={{0,4},{4,0},{8,12},{12,8},{16,20},{20,16},{24,28},{28,24},{1,5},{5... | collective-permute-start | bytes 786440 | tf_op jit(solution)/shard_map/ppermute | solution.py:496
  30.5 0.7 copy-start.5
  44.6 3.0 %copy-start.6 = (bf16[512,1024]{1,0:T(8,128)(2,1)}, bf16[512,1024]{1,0:T(8,128)(2,1)S(1)}, u32[]{:S(2)}) copy-start(bf16[512,1024]{1,0:T(8,128)(2,1)S(1)} %collective-permute-done.5.refs_3_) | copy-start | bytes 3145732
  44.6 3.0 %collective-permute-start.6 = (bf16[512,1024]{1,0:T(8,128)(2,1)S(1)}, bf16[512,1024]{1,0:T(8,128)(2,1)}, u32[]{:S(2)}, u32[]{:S(2)}) collective-permute-start(bf16[512,1024]{1,0:T(8,128)(2,1)S(1)} %collective-permute-done.5.refs_3_), channel_id=1, source_target_pairs={{0,4},{4,0},{8,12},{12,8},{16,20},{20,16},{24,28},{28,24},{1,5},{5... | collective-permute-start | bytes 3145736 | tf_op jit(solution)/shard_map/ppermute | solution.py:496
  44.8 15.6 %collective-permute-start.4 = (bf16[128,2048]{1,0:T(8,128)(2,1)}, bf16[128,2048]{1,0:T(8,128)(2,1)S(1)}, u32[]{:S(2)}, u32[]{:S(2)}) collective-permute-start(bf16[128,2048]{1,0:T(8,128)(2,1)} %get-tuple-element.32.refs_6_), channel_id=1, source_target_pairs={{0,4},{4,0},{8,12},{12,8},{16,20},{20,16},{24,28},{28,24},{1,5},{5... | collective-permute-start | bytes 1572872 | tf_op jit(solution)/shard_map/ppermute | solution.py:496
  45.1 15.2 %collective-permute-start.7 = (f32[3,128,1024]{2,1,0:T(8,128)}, f32[3,128,1024]{2,1,0:T(8,128)S(1)}, u32[]{:S(2)}, u32[]{:S(2)}) collective-permute-start(f32[3,128,1024]{2,1,0:T(8,128)} %get-tuple-element.38), channel_id=1, source_target_pairs={{0,4},{4,0},{8,12},{12,8},{16,20},{20,16},{24,28},{28,24},{1,5},{5... | collective-permute-start | bytes 4718600 | tf_op jit(solution)/shard_map/ppermute | solution.py:496
  45.3 15.1 %collective-permute-start.8 = (bf16[1024,2048]{1,0:T(8,128)(2,1)}, bf16[1024,2048]{1,0:T(8,128)(2,1)}, u32[]{:S(2)}, u32[]{:S(2)}) collective-permute-start(bf16[1024,2048]{1,0:T(8,128)(2,1)} %get-tuple-element.41.refs_15_), channel_id=1, source_target_pairs={{0,4},{4,0},{8,12},{12,8},{16,20},{20,16},{24,28},{28,24},{1,5},{5... | collective-permute-start | bytes 12582920 | tf_op jit(solution)/shard_map/ppermute | solution.py:496
  60.4 0.8 %copy-start.4 = (bf16[128,2048]{1,0:T(8,128)(2,1)}, bf16[128,2048]{1,0:T(8,128)(2,1)S(1)}, u32[]{:S(2)}) copy-start(bf16[128,2048]{1,0:T(8,128)(2,1)S(1)} %collective-permute-done.4.refs_7_) | copy-start | bytes 1572868
  60.4 1.3 %copy-start = (f32[3,128,1024]{2,1,0:T(8,128)}, f32[3,128,1024]{2,1,0:T(8,128)S(1)}, u32[]{:S(2)}) copy-start(f32[3,128,1024]{2,1,0:T(8,128)S(1)} %collective-permute-done.7.refs_12_) | copy-start | bytes 4718596

commit v4 on v3

--- a/solution.py
+++ b/solution.py
@@ -528,7 +528,9 @@
     )
     gother = exchange(gq, 1, 1)
     picks = pick_table(random_blocks, tokens.shape[0], shards)
-    kv_own, picks, *arrived[1:-1] = lax.optimization_barrier((kv_own, picks, *arrived[1:-1]))
+    kv_own, picks, gother, *arrived[1:-1] = lax.optimization_barrier(
+        (kv_own, picks, gother, *arrived[1:-1])
+    )
     if shards == 8:
         arrived[3] = exchange(arrived[1], 4, 2)
     kv_mine, g_mine, s_mine, s_other = rows_call(

time: 78.2 us -> 76.9 us (0.983)
  waiting for transfers between devices: 5.91 us -> 4.68 us
    ppermute x9, waiting for transfers between devices: 5.91 us -> 4.68 us  [exchange(): lax.ppermute(value, 'seq', [(i, i ^ (odd if i & 1 else even)) for i in ra...]
  transfers between devices with their start and end apart: 9 -> 9, of which waited for: 4 -> 3; matrix products, arithmetic and copies ran while one was open for 3% -> 3% of each run, Pallas kernels for 55% -> 56%
where the time goes in v4:
time: 76.9 us; the launch traced here: 76 us
  Pallas kernels  58.6 us (76%)
  starting transfers between devices  7.44 us (10%)
  waiting for transfers between devices  4.68 us (6%)
  local copies, waits for them, and re-layouts  2.46 us (3%)
  other arithmetic  1.85 us (2%)
  between operations  0.96 us (1%)
    pallas_call x4, Pallas kernels, call(): pl.pallas_call(kernel, out_shape=[jax.ShapeDtypeStruct(*out) for out in o...  58.6 us
    ppermute x9, starting transfers between devices, exchange(): lax.ppermute(value, 'seq', [(i, i ^ (odd if i & 1 else even)) for i in ra...  7.44 us
    ppermute x9, waiting for transfers between devices, exchange(): lax.ppermute(value, 'seq', [(i, i ^ (odd if i & 1 else even)) for i in ra...  4.68 us
    unnamed x14, local copies, waits for them, and re-layouts  2.3 us
  transfers between devices with their start and end apart: 9, of which 3 were waited for; matrix products, arithmetic and copies ran while one was open for 3% of the time, Pallas kernels for 56%

profile of v4, /device:TPU:0, one launch (start us, length us, event | category | flops | bytes accessed | tf_op | source)
XLA Modules:
  0.0 76.0 jit_solution(11508438088021694430)
XLA Ops:
  0.0 0.5 collective-permute-start
  0.5 2.5 %collective-permute-start.3 = (bf16[512,1024]{1,0:T(8,128)(2,1)}, bf16[512,1024]{1,0:T(8,128)(2,1)S(1)}, u32[]{:S(2)}, u32[]{:S(2)}) collective-permute-start(bf16[512,1024]{1,0:T(8,128)(2,1)} %refs_3_.1), channel_id=1, source_target_pairs={{0,16},{4,12},{8,24},{12,4},{16,0},{20,28},{24,8},{28,20},{1,17},{... | collective-permute-start | bytes 3145736 | tf_op jit(solution)/shard_map/ppermute | solution.py:496
  3.0 1.5 %collective-permute-start.2 = (bf16[512,1024]{1,0:T(8,128)(2,1)}, bf16[512,1024]{1,0:T(8,128)(2,1)S(1)}, u32[]{:S(2)}, u32[]{:S(2)}) collective-permute-start(bf16[512,1024]{1,0:T(8,128)(2,1)} %refs_3_.1), channel_id=1, source_target_pairs={{0,8},{4,20},{8,0},{12,28},{16,24},{20,4},{24,16},{28,12},{1,9},{5... | collective-permute-start | bytes 3145736 | tf_op jit(solution)/shard_map/ppermute | solution.py:496
  5.1 0.8 %negate_select_fusion = (s32[8,3]{0,1:T(4,128)S(1)}, s32[8,3]{0,1:T(4,128)S(1)}) fusion(s32[3]{0:T(128)S(1)} %iota_add_fusion, s32[8]{0:T(128)S(1)} %add_add_fusion, s32[64,3]{0,1:T(4,128)} %param.15, s32[]{:T(128)S(6)} %select_n.31), kind=kLoop, calls=%fused_computation.4 | loop fusion | flops 168 | bytes 336 | tf_op jit(solution)/shard_map/rem | solution.py:351
  5.9 0.1 copy.10
  6.0 0.1 reshape.18
  6.1 0.0 collective-permute-done.refs_4_
  6.1 0.0 copy-start.1
  6.1 1.0 %copy-done.1 = bf16[512,1024]{1,0:T(8,128)(2,1)} copy-done((bf16[512,1024]{1,0:T(8,128)(2,1)}, bf16[512,1024]{1,0:T(8,128)(2,1)S(1)}, u32[]{:S(2)}) %copy-start.1) | copy-done | bytes 1048600
  7.1 16.6 %first.1 = (bf16[1024,2048]{1,0:T(8,128)(2,1)}, bf16[128,2048]{1,0:T(8,128)(2,1)}, f32[3,128,1024]{2,1,0:T(8,128)}, bf16[512,1024]{1,0:T(8,128)(2,1)}, bf16[128,1024]{1,0:T(8,128)(2,1)}) custom-call(s32[1]{0:T(128)S(6)} %copy.11.refs_0_, s32[8,128]{1,0:T(8,128)} %refs_1_.7, f32[1,1024]{1,0:T(1,128)} %bitcast.1, bf16[512,1024]{1,0:T(8,128)(2,1)} %refs_3_.1, ...), custom_call_target="tpu_custom_call" | custom-call | flops 1024 | bytes 1024 | tf_op jit(solution)/shard_map/first/pallas_call | solution.py:298
  23.6 0.1 collective-permute-start.1
  23.7 0.6 multiply_add_fusion
  24.3 0.5 compare_select_fusion.6.refs_2_
  24.8 1.3 %collective-permute-done.3.refs_4_ = bf16[512,1024]{1,0:T(8,128)(2,1)S(1)} collective-permute-done((bf16[512,1024]{1,0:T(8,128)(2,1)}, bf16[512,1024]{1,0:T(8,128)(2,1)S(1)}, u32[]{:S(2)}, u32[]{:S(2)}) %collective-permute-start.3) | collective-permute-done | bytes 1048608 | tf_op jit(solution)/shard_map/ppermute | solution.py:496
  26.1 0.9 %collective-permute-done.2.refs_3_ = bf16[512,1024]{1,0:T(8,128)(2,1)S(1)} collective-permute-done((bf16[512,1024]{1,0:T(8,128)(2,1)}, bf16[512,1024]{1,0:T(8,128)(2,1)S(1)}, u32[]{:S(2)}, u32[]{:S(2)}) %collective-permute-start.2) | collective-permute-done | bytes 1048608 | tf_op jit(solution)/shard_map/ppermute | solution.py:496
  27.0 0.0 collective-permute-done.1.refs_8_
  27.0 1.8 %collective-permute-start.5 = (bf16[512,1024]{1,0:T(8,128)(2,1)S(1)}, bf16[512,1024]{1,0:T(8,128)(2,1)S(1)}, u32[]{:S(2)}, u32[]{:S(2)}) collective-permute-start(bf16[512,1024]{1,0:T(8,128)(2,1)S(1)} %collective-permute-done.2.refs_3_), channel_id=1, source_target_pairs={{0,16},{4,12},{8,24},{12,4},{16,0},{20,28},{24,8},{28,20},{1,17},{... | collective-permute-start | bytes 3145736 | tf_op jit(solution)/shard_map/ppermute | solution.py:496
  28.8 13.3 %middle.1 = (bf16[1024,2048]{1,0:T(8,128)(2,1)}, bf16[128,2048]{1,0:T(8,128)(2,1)}, f32[3,128,1024]{2,1,0:T(8,128)}, f32[3,128,1024]{2,1,0:T(8,128)}) custom-call(s32[1]{0:T(128)S(6)} %copy.11.refs_0_, s32[8,128]{1,0:T(8,128)} %refs_1_.7, f32[1,1024]{1,0:T(1,128)} %bitcast.2, bf16[512,1024]{1,0:T(8,128)(2,1)} %copy-done.3, bf16[512,1024]{1,0:T(8,128)(2,1)} %copy-done.2, ...), custom_call_target="tpu_custom_call" | custom-call | flops 1024 | bytes 1024 | tf_op jit(solution)/shard_map/middle/pallas_call | solution.py:298
  42.2 0.0 collective-permute-done.5.refs_3_
  42.2 0.0 copy-start.6
  42.2 0.1 collective-permute-start.6
  42.3 0.5 collective-permute-start.4
  42.8 0.1 collective-permute-start.7
  42.8 0.4 collective-permute-start.8
  43.3 2.5 %collective-permute-done.6.refs_4_ = bf16[512,1024]{1,0:T(8,128)(2,1)} collective-permute-done((bf16[512,1024]{1,0:T(8,128)(2,1)S(1)}, bf16[512,1024]{1,0:T(8,128)(2,1)}, u32[]{:S(2)}, u32[]{:S(2)}) %collective-permute-start.6) | collective-permute-done | bytes 1048608 | tf_op jit(solution)/shard_map/ppermute | solution.py:496
  45.7 12.8 %late.1 = (bf16[1024,2048]{1,0:T(8,128)(2,1)}, bf16[128,2048]{1,0:T(8,128)(2,1)}, f32[3,128,1024]{2,1,0:T(8,128)}) custom-call(s32[1]{0:T(128)S(6)} %copy.11.refs_0_, s32[8,128]{1,0:T(8,128)} %refs_1_.7, f32[1,1024]{1,0:T(1,128)} %bitcast.3, bf16[512,1024]{1,0:T(8,128)(2,1)} %copy-done.6, bf16[512,1024]{1,0:T(8,128)(2,1)} %collective-permute-done.6.refs_4_, ...), custom_call_target="tpu_custom_call" | custom-call | flops 99999997952 | bytes 1024 | tf_op jit(solution)/shard_map/late/pallas_call | solution.py:298
  58.6 0.0 collective-permute-done.4.refs_7_
  58.6 0.0 collective-permute-done.7.refs_12_
  58.6 0.0 collective-permute-done.8.refs_16_
  58.6 0.8 %copy-done.4 = bf16[128,2048]{1,0:T(8,128)(2,1)} copy-done((bf16[128,2048]{1,0:T(8,128)(2,1)}, bf16[128,2048]{1,0:T(8,128)(2,1)S(1)}, u32[]{:S(2)}) %copy-start.4) | copy-done | bytes 524312
  59.4 0.5 copy-done
  59.9 15.9 %attend.1 = bf16[512,1024]{1,0:T(8,128)(2,1)} custom-call(s32[1]{0:T(128)S(6)} %copy.11.refs_0_, s32[8,128]{1,0:T(8,128)} %refs_1_.7, s32[48]{0:T(128)} %compare_select_fusion.6.refs_2_, s32[48]{0:T(128)} %get-tuple-element.28.refs_3_, bf16[512,1024]{1,0:T(8,128)(2,1)} %get-tuple-element.29.refs_4_, bf16[128,2048]{1,0:T(8,128)(2,1)} %get-tuple-element.30.refs_5_, ...), custom_call_target="tpu_custom_call" | custom-call | flops 1024 | bytes 1024 | tf_op jit(solution)/shard_map/attend/pallas_call | solution.py:298
  (12 shorter events, 0.0 us)
Async XLA Ops:
  0.0 6.1 %collective-permute-start = (bf16[512,1024]{1,0:T(8,128)(2,1)}, bf16[512,1024]{1,0:T(8,128)(2,1)S(1)}, u32[]{:S(2)}, u32[]{:S(2)}) collective-permute-start(bf16[512,1024]{1,0:T(8,128)(2,1)} %refs_3_.1), channel_id=1, source_target_pairs={{0,4},{4,0},{8,12},{12,8},{16,20},{20,16},{24,28},{28,24},{1,5},{5... | collective-permute-start | bytes 3145736 | tf_op jit(solution)/shard_map/ppermute | solution.py:496
  0.5 25.7 %collective-permute-start.3 = (bf16[512,1024]{1,0:T(8,128)(2,1)}, bf16[512,1024]{1,0:T(8,128)(2,1)S(1)}, u32[]{:S(2)}, u32[]{:S(2)}) collective-permute-start(bf16[512,1024]{1,0:T(8,128)(2,1)} %refs_3_.1), channel_id=1, source_target_pairs={{0,16},{4,12},{8,24},{12,4},{16,0},{20,28},{24,8},{28,20},{1,17},{... | collective-permute-start | bytes 3145736 | tf_op jit(solution)/shard_map/ppermute | solution.py:496
  3.0 24.0 %collective-permute-start.2 = (bf16[512,1024]{1,0:T(8,128)(2,1)}, bf16[512,1024]{1,0:T(8,128)(2,1)S(1)}, u32[]{:S(2)}, u32[]{:S(2)}) collective-permute-start(bf16[512,1024]{1,0:T(8,128)(2,1)} %refs_3_.1), channel_id=1, source_target_pairs={{0,8},{4,20},{8,0},{12,28},{16,24},{20,4},{24,16},{28,12},{1,9},{5... | collective-permute-start | bytes 3145736 | tf_op jit(solution)/shard_map/ppermute | solution.py:496
  6.1 1.0 %copy-start.1 = (bf16[512,1024]{1,0:T(8,128)(2,1)}, bf16[512,1024]{1,0:T(8,128)(2,1)S(1)}, u32[]{:S(2)}) copy-start(bf16[512,1024]{1,0:T(8,128)(2,1)S(1)} %collective-permute-done.refs_4_) | copy-start | bytes 3145732
  23.6 3.3 %collective-permute-start.1 = (bf16[128,1024]{1,0:T(8,128)(2,1)}, bf16[128,1024]{1,0:T(8,128)(2,1)S(1)}, u32[]{:S(2)}, u32[]{:S(2)}) collective-permute-start(bf16[128,1024]{1,0:T(8,128)(2,1)} %get-tuple-element.26.refs_7_), channel_id=1, source_target_pairs={{0,4},{4,0},{8,12},{12,8},{16,20},{20,16},{24,28},{28,24},{1,5},{5... | collective-permute-start | bytes 786440 | tf_op jit(solution)/shard_map/ppermute | solution.py:496
  26.1 2.7 %copy-start.2 = (bf16[512,1024]{1,0:T(8,128)(2,1)}, bf16[512,1024]{1,0:T(8,128)(2,1)S(1)}, u32[]{:S(2)}) copy-start(bf16[512,1024]{1,0:T(8,128)(2,1)S(1)} %collective-permute-done.3.refs_4_) | copy-start | bytes 3145732
  27.0 1.8 %copy-start.3 = (bf16[512,1024]{1,0:T(8,128)(2,1)}, bf16[512,1024]{1,0:T(8,128)(2,1)S(1)}, u32[]{:S(2)}) copy-start(bf16[512,1024]{1,0:T(8,128)(2,1)S(1)} %collective-permute-done.2.refs_3_) | copy-start | bytes 3145732
  27.0 1.8 %copy-start.5 = (bf16[128,1024]{1,0:T(8,128)(2,1)}, bf16[128,1024]{1,0:T(8,128)(2,1)S(1)}, u32[]{:S(2)}) copy-start(bf16[128,1024]{1,0:T(8,128)(2,1)S(1)} %collective-permute-done.1.refs_8_) | copy-start | bytes 786436
  27.0 15.2 %collective-permute-start.5 = (bf16[512,1024]{1,0:T(8,128)(2,1)S(1)}, bf16[512,1024]{1,0:T(8,128)(2,1)S(1)}, u32[]{:S(2)}, u32[]{:S(2)}) collective-permute-start(bf16[512,1024]{1,0:T(8,128)(2,1)S(1)} %collective-permute-done.2.refs_3_), channel_id=1, source_target_pairs={{0,16},{4,12},{8,24},{12,4},{16,0},{20,28},{24,8},{28,20},{1,17},{... | collective-permute-start | bytes 3145736 | tf_op jit(solution)/shard_map/ppermute | solution.py:496
  42.2 3.6 %copy-start.6 = (bf16[512,1024]{1,0:T(8,128)(2,1)}, bf16[512,1024]{1,0:T(8,128)(2,1)S(1)}, u32[]{:S(2)}) copy-start(bf16[512,1024]{1,0:T(8,128)(2,1)S(1)} %collective-permute-done.5.refs_3_) | copy-start | bytes 3145732
  42.2 3.6 %collective-permute-start.6 = (bf16[512,1024]{1,0:T(8,128)(2,1)S(1)}, bf16[512,1024]{1,0:T(8,128)(2,1)}, u32[]{:S(2)}, u32[]{:S(2)}) collective-permute-start(bf16[512,1024]{1,0:T(8,128)(2,1)S(1)} %collective-permute-done.5.refs_3_), channel_id=1, source_target_pairs={{0,4},{4,0},{8,12},{12,8},{16,20},{20,16},{24,28},{28,24},{1,5},{5... | collective-permute-start | bytes 3145736 | tf_op jit(solution)/shard_map/ppermute | solution.py:496
  42.3 16.3 %collective-permute-start.4 = (bf16[128,2048]{1,0:T(8,128)(2,1)}, bf16[128,2048]{1,0:T(8,128)(2,1)S(1)}, u32[]{:S(2)}, u32[]{:S(2)}) collective-permute-start(bf16[128,2048]{1,0:T(8,128)(2,1)} %get-tuple-element.34.refs_6_), channel_id=1, source_target_pairs={{0,4},{4,0},{8,12},{12,8},{16,20},{20,16},{24,28},{28,24},{1,5},{5... | collective-permute-start | bytes 1572872 | tf_op jit(solution)/shard_map/ppermute | solution.py:496
  42.8 15.8 %collective-permute-start.7 = (f32[3,128,1024]{2,1,0:T(8,128)}, f32[3,128,1024]{2,1,0:T(8,128)S(1)}, u32[]{:S(2)}, u32[]{:S(2)}) collective-permute-start(f32[3,128,1024]{2,1,0:T(8,128)} %get-tuple-element.40), channel_id=1, source_target_pairs={{0,4},{4,0},{8,12},{12,8},{16,20},{20,16},{24,28},{28,24},{1,5},{5... | collective-permute-start | bytes 4718600 | tf_op jit(solution)/shard_map/ppermute | solution.py:496
  42.8 15.8 %collective-permute-start.8 = (bf16[1024,2048]{1,0:T(8,128)(2,1)}, bf16[1024,2048]{1,0:T(8,128)(2,1)}, u32[]{:S(2)}, u32[]{:S(2)}) collective-permute-start(bf16[1024,2048]{1,0:T(8,128)(2,1)} %get-tuple-element.43.refs_15_), channel_id=1, source_target_pairs={{0,4},{4,0},{8,12},{12,8},{16,20},{20,16},{24,28},{28,24},{1,5},{5... | collective-permute-start | bytes 12582920 | tf_op jit(solution)/shard_map/ppermute | solution.py:496
  58.6 0.8 %copy-start.4 = (bf16[128,2048]{1,0:T(8,128)(2,1)}, bf16[128,2048]{1,0:T(8,128)(2,1)S(1)}, u32[]{:S(2)}) copy-start(bf16[128,2048]{1,0:T(8,128)(2,1)S(1)} %collective-permute-done.4.refs_7_) | copy-start | bytes 1572868
  58.6 1.3 %copy-start = (f32[3,128,1024]{2,1,0:T(8,128)}, f32[3,128,1024]{2,1,0:T(8,128)S(1)}, u32[]{:S(2)}) copy-start(f32[3,128,1024]{2,1,0:T(8,128)S(1)} %collective-permute-done.7.refs_12_) | copy-start | bytes 4718596

commit v5 on v4

--- a/solution.py
+++ b/solution.py
@@ -377,6 +377,10 @@
             if act == "wait":
                 pltpu.make_async_copy(kv_refs[0].at[pl.ds(0, BLOCK), :], target, sem).wait()
                 continue
+            if pick == 1:
+                own = pl.ds(pl.multiple_of(block * BLOCK, BLOCK), BLOCK)
+                pltpu.make_async_copy(kv_refs[0].at[own, :], target, sem).start()
+                continue
             entry = block * PICKS + pick
             source = source_ref[entry]
             start = pl.multiple_of(start_ref[entry], BLOCK)
@@ -402,8 +406,7 @@
     keys[0, span:, :] = gathered
     keys[1, span:, :] = gathered
 
-    def one_block(block, carry):
-        slot = lax.rem(block, 2)
+    def one_block(block, slot):
 
         @pl.when(block + 1 < blocks)
         def _():
@@ -435,9 +438,13 @@
             mixed[at, g * GW : (g + 1) * GW] = pick_heads(
                 weighted * (1.0 / totals[g]), BLOCK
             ).astype(BF16)
+
+    def two_blocks(step, carry):
+        one_block(2 * step, 0)
+        one_block(2 * step + 1, 1)
         return carry
 
-    lax.fori_loop(0, blocks, one_block, 0)
+    lax.fori_loop(0, blocks // 2, two_blocks, 0)
     move_state(info.tiles, pairs, state_sems, "wait")
     merge_states(info.tiles, mine_refs, placed)
     row = lax.broadcasted_iota(jnp.int32, (rows, NGLOB), 0)

time: 76.9 us -> 76.9 us (level)
  no operation moved by 1% of the time
where the time goes in v5:
time: 76.9 us; the launch traced here: 76 us
  Pallas kernels  58.6 us (76%)
  starting transfers between devices  7.44 us (10%)
  waiting for transfers between devices  4.68 us (6%)
  local copies, waits for them, and re-layouts  2.46 us (3%)
  other arithmetic  1.85 us (2%)
  between operations  0.96 us (1%)
    pallas_call x4, Pallas kernels, call(): pl.pallas_call(kernel, out_shape=[jax.ShapeDtypeStruct(*out) for out in o...  58.6 us
    ppermute x9, starting transfers between devices, exchange(): lax.ppermute(value, 'seq', [(i, i ^ (odd if i & 1 else even)) for i in ra...  7.44 us
    ppermute x9, waiting for transfers between devices, exchange(): lax.ppermute(value, 'seq', [(i, i ^ (odd if i & 1 else even)) for i in ra...  4.68 us
    unnamed x14, local copies, waits for them, and re-layouts  2.3 us
  transfers between devices with their start and end apart: 9, of which 3 were waited for; matrix products, arithmetic and copies ran while one was open for 3% of the time, Pallas kernels for 56%

profile of v5, /device:TPU:0, one launch (start us, length us, event | category | flops | bytes accessed | tf_op | source)
XLA Modules:
  0.0 76.0 jit_solution(9106685281918342248)
XLA Ops:
  0.0 0.5 collective-permute-start
  0.5 2.5 %collective-permute-start.3 = (bf16[512,1024]{1,0:T(8,128)(2,1)}, bf16[512,1024]{1,0:T(8,128)(2,1)S(1)}, u32[]{:S(2)}, u32[]{:S(2)}) collective-permute-start(bf16[512,1024]{1,0:T(8,128)(2,1)} %refs_3_.1), channel_id=1, source_target_pairs={{0,16},{4,12},{8,24},{12,4},{16,0},{20,28},{24,8},{28,20},{1,17},{... | collective-permute-start | bytes 3145736 | tf_op jit(solution)/shard_map/ppermute | solution.py:503
  3.0 1.5 %collective-permute-start.2 = (bf16[512,1024]{1,0:T(8,128)(2,1)}, bf16[512,1024]{1,0:T(8,128)(2,1)S(1)}, u32[]{:S(2)}, u32[]{:S(2)}) collective-permute-start(bf16[512,1024]{1,0:T(8,128)(2,1)} %refs_3_.1), channel_id=1, source_target_pairs={{0,8},{4,20},{8,0},{12,28},{16,24},{20,4},{24,16},{28,12},{1,9},{5... | collective-permute-start | bytes 3145736 | tf_op jit(solution)/shard_map/ppermute | solution.py:503
  5.1 0.8 %negate_select_fusion = (s32[8,3]{0,1:T(4,128)S(1)}, s32[8,3]{0,1:T(4,128)S(1)}) fusion(s32[3]{0:T(128)S(1)} %iota_add_fusion, s32[8]{0:T(128)S(1)} %add_add_fusion, s32[64,3]{0,1:T(4,128)} %param.15, s32[]{:T(128)S(6)} %select_n.31), kind=kLoop, calls=%fused_computation.4 | loop fusion | flops 168 | bytes 336 | tf_op jit(solution)/shard_map/rem | solution.py:351
  5.9 0.1 copy.10
  6.0 0.1 reshape.18
  6.1 0.0 collective-permute-done.refs_4_
  6.1 0.0 copy-start.1
  6.1 1.0 %copy-done.1 = bf16[512,1024]{1,0:T(8,128)(2,1)} copy-done((bf16[512,1024]{1,0:T(8,128)(2,1)}, bf16[512,1024]{1,0:T(8,128)(2,1)S(1)}, u32[]{:S(2)}) %copy-start.1) | copy-done | bytes 1048600
  7.1 16.6 %first.1 = (bf16[1024,2048]{1,0:T(8,128)(2,1)}, bf16[128,2048]{1,0:T(8,128)(2,1)}, f32[3,128,1024]{2,1,0:T(8,128)}, bf16[512,1024]{1,0:T(8,128)(2,1)}, bf16[128,1024]{1,0:T(8,128)(2,1)}) custom-call(s32[1]{0:T(128)S(6)} %copy.11.refs_0_, s32[8,128]{1,0:T(8,128)} %refs_1_.7, f32[1,1024]{1,0:T(1,128)} %bitcast.1, bf16[512,1024]{1,0:T(8,128)(2,1)} %refs_3_.1, ...), custom_call_target="tpu_custom_call" | custom-call | flops 1024 | bytes 1024 | tf_op jit(solution)/shard_map/first/pallas_call | solution.py:298
  23.6 0.1 collective-permute-start.1
  23.7 0.6 multiply_add_fusion
  24.3 0.5 compare_select_fusion.6.refs_2_
  24.8 1.3 %collective-permute-done.3.refs_4_ = bf16[512,1024]{1,0:T(8,128)(2,1)S(1)} collective-permute-done((bf16[512,1024]{1,0:T(8,128)(2,1)}, bf16[512,1024]{1,0:T(8,128)(2,1)S(1)}, u32[]{:S(2)}, u32[]{:S(2)}) %collective-permute-start.3) | collective-permute-done | bytes 1048608 | tf_op jit(solution)/shard_map/ppermute | solution.py:503
  26.1 0.9 %collective-permute-done.2.refs_3_ = bf16[512,1024]{1,0:T(8,128)(2,1)S(1)} collective-permute-done((bf16[512,1024]{1,0:T(8,128)(2,1)}, bf16[512,1024]{1,0:T(8,128)(2,1)S(1)}, u32[]{:S(2)}, u32[]{:S(2)}) %collective-permute-start.2) | collective-permute-done | bytes 1048608 | tf_op jit(solution)/shard_map/ppermute | solution.py:503
  27.0 0.0 collective-permute-done.1.refs_8_
  27.0 1.8 %collective-permute-start.5 = (bf16[512,1024]{1,0:T(8,128)(2,1)S(1)}, bf16[512,1024]{1,0:T(8,128)(2,1)S(1)}, u32[]{:S(2)}, u32[]{:S(2)}) collective-permute-start(bf16[512,1024]{1,0:T(8,128)(2,1)S(1)} %collective-permute-done.2.refs_3_), channel_id=1, source_target_pairs={{0,16},{4,12},{8,24},{12,4},{16,0},{20,28},{24,8},{28,20},{1,17},{... | collective-permute-start | bytes 3145736 | tf_op jit(solution)/shard_map/ppermute | solution.py:503
  28.8 13.3 %middle.1 = (bf16[1024,2048]{1,0:T(8,128)(2,1)}, bf16[128,2048]{1,0:T(8,128)(2,1)}, f32[3,128,1024]{2,1,0:T(8,128)}, f32[3,128,1024]{2,1,0:T(8,128)}) custom-call(s32[1]{0:T(128)S(6)} %copy.11.refs_0_, s32[8,128]{1,0:T(8,128)} %refs_1_.7, f32[1,1024]{1,0:T(1,128)} %bitcast.2, bf16[512,1024]{1,0:T(8,128)(2,1)} %copy-done.3, bf16[512,1024]{1,0:T(8,128)(2,1)} %copy-done.2, ...), custom_call_target="tpu_custom_call" | custom-call | flops 1024 | bytes 1024 | tf_op jit(solution)/shard_map/middle/pallas_call | solution.py:298
  42.2 0.0 collective-permute-done.5.refs_3_
  42.2 0.0 copy-start.6
  42.2 0.1 collective-permute-start.6
  42.3 0.5 collective-permute-start.4
  42.8 0.1 collective-permute-start.7
  42.8 0.4 collective-permute-start.8
  43.3 2.5 %collective-permute-done.6.refs_4_ = bf16[512,1024]{1,0:T(8,128)(2,1)} collective-permute-done((bf16[512,1024]{1,0:T(8,128)(2,1)S(1)}, bf16[512,1024]{1,0:T(8,128)(2,1)}, u32[]{:S(2)}, u32[]{:S(2)}) %collective-permute-start.6) | collective-permute-done | bytes 1048608 | tf_op jit(solution)/shard_map/ppermute | solution.py:503
  45.7 12.8 %late.1 = (bf16[1024,2048]{1,0:T(8,128)(2,1)}, bf16[128,2048]{1,0:T(8,128)(2,1)}, f32[3,128,1024]{2,1,0:T(8,128)}) custom-call(s32[1]{0:T(128)S(6)} %copy.11.refs_0_, s32[8,128]{1,0:T(8,128)} %refs_1_.7, f32[1,1024]{1,0:T(1,128)} %bitcast.3, bf16[512,1024]{1,0:T(8,128)(2,1)} %copy-done.6, bf16[512,1024]{1,0:T(8,128)(2,1)} %collective-permute-done.6.refs_4_, ...), custom_call_target="tpu_custom_call" | custom-call | flops 99999997952 | bytes 1024 | tf_op jit(solution)/shard_map/late/pallas_call | solution.py:298
  58.6 0.0 collective-permute-done.4.refs_7_
  58.6 0.0 collective-permute-done.7.refs_12_
  58.6 0.0 collective-permute-done.8.refs_16_
  58.6 0.8 %copy-done.4 = bf16[128,2048]{1,0:T(8,128)(2,1)} copy-done((bf16[128,2048]{1,0:T(8,128)(2,1)}, bf16[128,2048]{1,0:T(8,128)(2,1)S(1)}, u32[]{:S(2)}) %copy-start.4) | copy-done | bytes 524312
  59.4 0.5 copy-done
  59.9 15.9 %attend.1 = bf16[512,1024]{1,0:T(8,128)(2,1)} custom-call(s32[1]{0:T(128)S(6)} %copy.11.refs_0_, s32[8,128]{1,0:T(8,128)} %refs_1_.7, s32[48]{0:T(128)} %compare_select_fusion.6.refs_2_, s32[48]{0:T(128)} %get-tuple-element.28.refs_3_, bf16[512,1024]{1,0:T(8,128)(2,1)} %get-tuple-element.29.refs_4_, bf16[128,2048]{1,0:T(8,128)(2,1)} %get-tuple-element.30.refs_5_, ...), custom_call_target="tpu_custom_call" | custom-call | flops 1024 | bytes 1024 | tf_op jit(solution)/shard_map/attend/pallas_call | solution.py:298
  (12 shorter events, 0.0 us)
Async XLA Ops:
  0.0 6.1 %collective-permute-start = (bf16[512,1024]{1,0:T(8,128)(2,1)}, bf16[512,1024]{1,0:T(8,128)(2,1)S(1)}, u32[]{:S(2)}, u32[]{:S(2)}) collective-permute-start(bf16[512,1024]{1,0:T(8,128)(2,1)} %refs_3_.1), channel_id=1, source_target_pairs={{0,4},{4,0},{8,12},{12,8},{16,20},{20,16},{24,28},{28,24},{1,5},{5... | collective-permute-start | bytes 3145736 | tf_op jit(solution)/shard_map/ppermute | solution.py:503
  0.5 25.7 %collective-permute-start.3 = (bf16[512,1024]{1,0:T(8,128)(2,1)}, bf16[512,1024]{1,0:T(8,128)(2,1)S(1)}, u32[]{:S(2)}, u32[]{:S(2)}) collective-permute-start(bf16[512,1024]{1,0:T(8,128)(2,1)} %refs_3_.1), channel_id=1, source_target_pairs={{0,16},{4,12},{8,24},{12,4},{16,0},{20,28},{24,8},{28,20},{1,17},{... | collective-permute-start | bytes 3145736 | tf_op jit(solution)/shard_map/ppermute | solution.py:503
  3.0 24.0 %collective-permute-start.2 = (bf16[512,1024]{1,0:T(8,128)(2,1)}, bf16[512,1024]{1,0:T(8,128)(2,1)S(1)}, u32[]{:S(2)}, u32[]{:S(2)}) collective-permute-start(bf16[512,1024]{1,0:T(8,128)(2,1)} %refs_3_.1), channel_id=1, source_target_pairs={{0,8},{4,20},{8,0},{12,28},{16,24},{20,4},{24,16},{28,12},{1,9},{5... | collective-permute-start | bytes 3145736 | tf_op jit(solution)/shard_map/ppermute | solution.py:503
  6.1 1.0 %copy-start.1 = (bf16[512,1024]{1,0:T(8,128)(2,1)}, bf16[512,1024]{1,0:T(8,128)(2,1)S(1)}, u32[]{:S(2)}) copy-start(bf16[512,1024]{1,0:T(8,128)(2,1)S(1)} %collective-permute-done.refs_4_) | copy-start | bytes 3145732
  23.6 3.3 %collective-permute-start.1 = (bf16[128,1024]{1,0:T(8,128)(2,1)}, bf16[128,1024]{1,0:T(8,128)(2,1)S(1)}, u32[]{:S(2)}, u32[]{:S(2)}) collective-permute-start(bf16[128,1024]{1,0:T(8,128)(2,1)} %get-tuple-element.26.refs_7_), channel_id=1, source_target_pairs={{0,4},{4,0},{8,12},{12,8},{16,20},{20,16},{24,28},{28,24},{1,5},{5... | collective-permute-start | bytes 786440 | tf_op jit(solution)/shard_map/ppermute | solution.py:503
  26.1 2.7 %copy-start.2 = (bf16[512,1024]{1,0:T(8,128)(2,1)}, bf16[512,1024]{1,0:T(8,128)(2,1)S(1)}, u32[]{:S(2)}) copy-start(bf16[512,1024]{1,0:T(8,128)(2,1)S(1)} %collective-permute-done.3.refs_4_) | copy-start | bytes 3145732
  27.0 1.8 %copy-start.3 = (bf16[512,1024]{1,0:T(8,128)(2,1)}, bf16[512,1024]{1,0:T(8,128)(2,1)S(1)}, u32[]{:S(2)}) copy-start(bf16[512,1024]{1,0:T(8,128)(2,1)S(1)} %collective-permute-done.2.refs_3_) | copy-start | bytes 3145732
  27.0 1.8 %copy-start.5 = (bf16[128,1024]{1,0:T(8,128)(2,1)}, bf16[128,1024]{1,0:T(8,128)(2,1)S(1)}, u32[]{:S(2)}) copy-start(bf16[128,1024]{1,0:T(8,128)(2,1)S(1)} %collective-permute-done.1.refs_8_) | copy-start | bytes 786436
  27.0 15.2 %collective-permute-start.5 = (bf16[512,1024]{1,0:T(8,128)(2,1)S(1)}, bf16[512,1024]{1,0:T(8,128)(2,1)S(1)}, u32[]{:S(2)}, u32[]{:S(2)}) collective-permute-start(bf16[512,1024]{1,0:T(8,128)(2,1)S(1)} %collective-permute-done.2.refs_3_), channel_id=1, source_target_pairs={{0,16},{4,12},{8,24},{12,4},{16,0},{20,28},{24,8},{28,20},{1,17},{... | collective-permute-start | bytes 3145736 | tf_op jit(solution)/shard_map/ppermute | solution.py:503
  42.2 3.6 %copy-start.6 = (bf16[512,1024]{1,0:T(8,128)(2,1)}, bf16[512,1024]{1,0:T(8,128)(2,1)S(1)}, u32[]{:S(2)}) copy-start(bf16[512,1024]{1,0:T(8,128)(2,1)S(1)} %collective-permute-done.5.refs_3_) | copy-start | bytes 3145732
  42.2 3.6 %collective-permute-start.6 = (bf16[512,1024]{1,0:T(8,128)(2,1)S(1)}, bf16[512,1024]{1,0:T(8,128)(2,1)}, u32[]{:S(2)}, u32[]{:S(2)}) collective-permute-start(bf16[512,1024]{1,0:T(8,128)(2,1)S(1)} %collective-permute-done.5.refs_3_), channel_id=1, source_target_pairs={{0,4},{4,0},{8,12},{12,8},{16,20},{20,16},{24,28},{28,24},{1,5},{5... | collective-permute-start | bytes 3145736 | tf_op jit(solution)/shard_map/ppermute | solution.py:503
  42.3 16.3 %collective-permute-start.4 = (bf16[128,2048]{1,0:T(8,128)(2,1)}, bf16[128,2048]{1,0:T(8,128)(2,1)S(1)}, u32[]{:S(2)}, u32[]{:S(2)}) collective-permute-start(bf16[128,2048]{1,0:T(8,128)(2,1)} %get-tuple-element.34.refs_6_), channel_id=1, source_target_pairs={{0,4},{4,0},{8,12},{12,8},{16,20},{20,16},{24,28},{28,24},{1,5},{5... | collective-permute-start | bytes 1572872 | tf_op jit(solution)/shard_map/ppermute | solution.py:503
  42.8 15.8 %collective-permute-start.7 = (f32[3,128,1024]{2,1,0:T(8,128)}, f32[3,128,1024]{2,1,0:T(8,128)S(1)}, u32[]{:S(2)}, u32[]{:S(2)}) collective-permute-start(f32[3,128,1024]{2,1,0:T(8,128)} %get-tuple-element.40), channel_id=1, source_target_pairs={{0,4},{4,0},{8,12},{12,8},{16,20},{20,16},{24,28},{28,24},{1,5},{5... | collective-permute-start | bytes 4718600 | tf_op jit(solution)/shard_map/ppermute | solution.py:503
  42.8 15.8 %collective-permute-start.8 = (bf16[1024,2048]{1,0:T(8,128)(2,1)}, bf16[1024,2048]{1,0:T(8,128)(2,1)}, u32[]{:S(2)}, u32[]{:S(2)}) collective-permute-start(bf16[1024,2048]{1,0:T(8,128)(2,1)} %get-tuple-element.43.refs_15_), channel_id=1, source_target_pairs={{0,4},{4,0},{8,12},{12,8},{16,20},{20,16},{24,28},{28,24},{1,5},{5... | collective-permute-start | bytes 12582920 | tf_op jit(solution)/shard_map/ppermute | solution.py:503
  58.6 0.8 %copy-start.4 = (bf16[128,2048]{1,0:T(8,128)(2,1)}, bf16[128,2048]{1,0:T(8,128)(2,1)S(1)}, u32[]{:S(2)}) copy-start(bf16[128,2048]{1,0:T(8,128)(2,1)S(1)} %collective-permute-done.4.refs_7_) | copy-start | bytes 1572868
  58.6 1.3 %copy-start = (f32[3,128,1024]{2,1,0:T(8,128)}, f32[3,128,1024]{2,1,0:T(8,128)S(1)}, u32[]{:S(2)}) copy-start(f32[3,128,1024]{2,1,0:T(8,128)S(1)} %collective-permute-done.7.refs_12_) | copy-start | bytes 4718596
